TPU v7x, 128 devices: a whole 4x4x4 slice. The times are simulated.
128 devices in a mesh: gx: 8 (over y, x_hi), gy: 16 (over z, x_lo, core).
Axes of the slice: x: 4 (x_hi: 2, x_lo: 2; x = x_hi * 2 + x_lo), y: 4, z: 4, core: 2. Of those that a mesh axis runs over, the one named last changes fastest.
Arguments:
- displacement: float32 [3, 128, 256, 128], P(None, 'gy', 'gx'), may hold values from -0.25 to 0.25
- volume: float32 [128, 256, 128], P('gy', 'gx'), may hold values from 0.5 to 2
- material: int32 [128, 256], P('gy', 'gx'), may hold values from 0 to 1, as said below
- layers: int32 [128, 256], P('gy', 'gx'), may hold values from 126 to 128
Outputs:
- factors: float32 [3, 128, 256, 128], P(None, 'gy', 'gx')
- force: float32 [3, 128, 256, 128], P(None, 'gy', 'gx')
Inputs may be any that keep to these rules, and one draw needn't show every extreme that they name: `material`: A slit two rows wide, cut from the plate's edge x = 0 into the plate, is 0, and scattered further columns are 0; all others are 1.
All inputs are finite; a program needn't handle non-finite values.
Results may differ from a plain program's by a relative error of at most 0.0003.
Values sent between devices are 32-bit elements; how exact they have to be, the bound alone decides.
A program may use at most 128 MiB of HBM per device.

v0:
```python
import functools
import math

import jax
import jax.numpy as jnp
from jax import lax
from jax.experimental import pallas as pl
from jax.experimental.pallas import tpu as pltpu
from jax.sharding import PartitionSpec as P

HORIZON = 3
STIFF = 5.0
WIDE = 2 * HORIZON
LANES = 128
SUB = 8
MESH = pl.DeviceIdType.MESH
SIDES = (-1, 1)
STEPS = tuple((dx, dy) for dy in (-1, 0, 1) for dx in (-1, 0, 1) if (dx, dy) != (0, 0))
CORNERS = tuple(step for step in STEPS if step[0] and step[1])


def bond_list():
    reach = range(-HORIZON, HORIZON + 1)
    return [
        (x, y, z)
        for y in reach
        for x in reach
        for z in reach
        if 0 < x * x + y * y + z * z <= HORIZON * HORIZON
    ]


def bond_types():
    kinds = {}
    for bond in bond_list():
        kinds.setdefault(tuple(sorted(map(abs, bond))), []).append(bond)
    return kinds


def influence(square):
    return (1.0 - square / (HORIZON * HORIZON)) ** 2


def pair_list():
    reach = range(HORIZON + 1)
    return [(ax, az) for ax in reach for az in reach if ax * ax + az * az <= HORIZON * HORIZON]


TPAIRS = [pair for pair in pair_list() if pair[0] > 0]


def shifted(value, step):
    return pltpu.roll(value, (-step) % LANES, 1) if step else value


def kernel(
    disp, volume, material, layers, fac_out, force_out,
    vol_ext, mirror, mirror_x, ext, send_x, send_c, got_y, got_x, got_c, sems,
):
    rows, cols = volume.shape[0], volume.shape[1]
    left = SUB
    gx, gy = lax.axis_index("gx"), lax.axis_index("gy")
    nx, ny = lax.axis_size("gx"), lax.axis_size("gy")

    def has(step):
        dx, dy = step
        found = None
        for delta, at, size in ((dx, gx, nx), (dy, gy, ny)):
            if delta:
                test = at > 0 if delta < 0 else at < size - 1
                found = test if found is None else found & test
        return found

    def device(step):
        return {"gx": gx + step[0], "gy": gy + step[1]}

    barrier = pltpu.get_barrier_semaphore()
    for step in STEPS:

        @pl.when(has(step))
        def _():
            pl.semaphore_signal(barrier, inc=1, device_id=device(step), device_id_type=MESH)

    lane = lax.broadcasted_iota(jnp.int32, (SUB, LANES), 1)
    sub = lax.broadcasted_iota(jnp.int32, (SUB, LANES), 0)
    sub_f = sub.astype(jnp.float32)
    zero = jnp.zeros((SUB, LANES), jnp.float32)

    eye_row = lax.broadcasted_iota(jnp.int32, (cols, cols), 0)
    eye_col = lax.broadcasted_iota(jnp.int32, (cols, cols), 1)
    level = lax.broadcasted_iota(jnp.int32, (cols, LANES), 1).astype(jnp.float32)
    filled = jnp.where(material[...] > 0, layers[...], 0).astype(jnp.float32)
    for y in range(rows):
        line = jnp.broadcast_to(filled[y : y + 1, :], (cols, cols))
        top = jnp.sum(jnp.where(eye_row == eye_col, line, 0.0), axis=1, keepdims=True)
        vol_ext[WIDE + y, left : left + cols, :] = jnp.where(
            level < jnp.broadcast_to(top, (cols, LANES)), volume[y], 0.0
        )

    for side, first in ((0, 0), (1, cols - HORIZON)):
        for k in range(3):
            for y in range(rows):
                at = (k * rows + y) * HORIZON
                send_x[side, at : at + HORIZON, :] = disp[k, y, first : first + HORIZON, :]
    for index, (dx, dy) in enumerate(CORNERS):
        first = 0 if dx < 0 else cols - HORIZON
        start = 0 if dy < 0 else rows - HORIZON
        for k in range(3):
            for y in range(HORIZON):
                at = (k * HORIZON + y) * HORIZON
                send_c[index, at : at + HORIZON, :] = disp[k, start + y, first : first + HORIZON, :]

    right = left + cols
    bottom = WIDE + rows

    def clear(ref, *where):
        ref[where] = jnp.zeros(ref.at[where].shape, jnp.float32)

    @pl.when(gx == 0)
    def _():
        clear(vol_ext, slice(None), slice(0, left))
        clear(got_x, 0)

    @pl.when(gx == nx - 1)
    def _():
        clear(vol_ext, slice(None), slice(right, right + SUB))
        clear(got_x, 1)

    @pl.when(gy == 0)
    def _():
        clear(vol_ext, slice(0, WIDE))
        clear(got_y, 0)

    @pl.when(gy == ny - 1)
    def _():
        clear(vol_ext, slice(bottom, bottom + WIDE))
        clear(got_y, 1)

    for index, step in enumerate(CORNERS):

        @pl.when(jnp.logical_not(has(step)))
        def _():
            clear(got_c, index)

    peers = sum(has(step).astype(jnp.int32) for step in STEPS)
    pl.semaphore_wait(barrier, peers)

    def cut_from(delta, size, width):
        return {-1: (0, width), 0: (0, size), 1: (size - width, width)}[delta]

    def vol_copy(step):
        dx, dy = step
        y0, yn = cut_from(dy, rows, WIDE)
        x0, xn = cut_from(dx, cols, SUB)
        to_y = {-1: bottom, 0: WIDE, 1: 0}[dy]
        to_x = {-1: right, 0: left, 1: 0}[dx]
        slot = STEPS.index(step)
        return pltpu.make_async_remote_copy(
            src_ref=vol_ext.at[WIDE + y0 : WIDE + y0 + yn, left + x0 : left + x0 + xn],
            dst_ref=vol_ext.at[to_y : to_y + yn, to_x : to_x + xn],
            send_sem=sems.at[0, slot],
            recv_sem=sems.at[1, STEPS.index((-dx, -dy))],
            device_id=device(step),
            device_id_type=MESH,
        )

    def disp_copy(step):
        dx, dy = step
        slot = STEPS.index(step)
        if dx == 0:
            y0, yn = cut_from(dy, rows, HORIZON)
            source, target = disp.at[:, y0 : y0 + yn], got_y.at[0 if dy > 0 else 1]
        elif dy == 0:
            source, target = send_x.at[0 if dx < 0 else 1], got_x.at[0 if dx > 0 else 1]
        else:
            source, target = send_c.at[CORNERS.index(step)], got_c.at[CORNERS.index((-dx, -dy))]
        return pltpu.make_async_remote_copy(
            src_ref=source,
            dst_ref=target,
            send_sem=sems.at[2, slot],
            recv_sem=sems.at[3, STEPS.index((-dx, -dy))],
            device_id=device(step),
            device_id_type=MESH,
        )

    order = sorted(STEPS, key=lambda step: (-abs(step[0]) - abs(step[1]), -abs(step[0])))
    for make in (vol_copy, disp_copy):
        for step in order:

            @pl.when(has(step))
            def _():
                make(step).start()

    def arrived(make, step):
        @pl.when(has(step))
        def _():
            dx, dy = step
            make((-dx, -dy)).wait_recv()

    def put(k, y, at, value):
        width = value.shape[0]
        for oz in range(-2, 3):
            moved = shifted(value, oz)
            if k == 2 and oz:
                moved = moved + float(oz)
            ext[k * 5 + oz + 2, y, pl.ds(at, width), :] = moved

    middle_x = left + cols // 2
    middle_y = HORIZON + rows // 2

    def position(k, value, y, at):
        if k == 0:
            index = sub_f[: value.shape[0]] if value.shape[0] < SUB else sub_f
            return value + (index + float(at - middle_x))
        if k == 1:
            return value + (y - middle_y).astype(jnp.float32)
        return value

    def own_row(y, carry):
        for k in range(3):
            for at in range(0, cols, SUB):
                value = position(k, disp[k, y, at : at + SUB, :], y + HORIZON, left + at)
                put(k, y + HORIZON, left + at, value)
        return carry

    lax.fori_loop(0, rows, own_row, 0)

    for step in order:
        arrived(vol_copy, step)

    def mirror_row(r, carry):
        for at in range(0, right + SUB, SUB):
            value = vol_ext[r, at : at + SUB, :]
            parts = []
            for a in range(1, HORIZON + 1):
                ahead = jnp.where(lane < LANES - a, shifted(value, a), 0.0)
                behind = jnp.where(lane >= a, shifted(value, -a), 0.0)
                mirror[a - 1, r, at : at + SUB, :] = ahead + behind
                parts.append((ahead, behind))

            @pl.when((r >= HORIZON) & (r < HORIZON + ext.shape[1]))
            def _():
                ext[6 * 5 + 2, r - HORIZON, at : at + SUB, :] = value
                for a in (1, 2):
                    ext[6 * 5 + 2 + a, r - HORIZON, at : at + SUB, :] = parts[a - 1][0]
                    ext[6 * 5 + 2 - a, r - HORIZON, at : at + SUB, :] = parts[a - 1][1]

        for tile in range(mirror_x.shape[2] // SUB):
            at = left - HORIZON + tile * SUB
            for index, (ax, az) in enumerate(TPAIRS):
                total = side_sum(az, r, at + ax) + side_sum(az, r, at - ax)
                mirror_x[index, r, tile * SUB : tile * SUB + SUB, :] = total
        return carry

    def side_sum(az, r, at):
        if az == 0:
            return vol_ext[r, at : at + SUB, :]
        return mirror[az - 1, r, at : at + SUB, :]

    lax.fori_loop(0, vol_ext.shape[0], mirror_row, 0)

    bulk = math.pi * HORIZON**4 / 30.0

    def factor_row(y, carry):
        r = y + HORIZON
        for tile in range(mirror_x.shape[2] // SUB):
            at = left - HORIZON + tile * SUB

            def pick(ax, az, row):
                if ax:
                    return mirror_x[TPAIRS.index((ax, az)), row, tile * SUB : tile * SUB + SUB, :]
                return side_sum(az, row, at)

            energy = [zero, zero, zero]
            for ax, az in pair_list():
                for ay in range(HORIZON + 1):
                    square = ax * ax + ay * ay + az * az
                    if not 0 < square <= HORIZON * HORIZON:
                        continue
                    total = pick(ax, az, r + ay)
                    if ay:
                        total = total + pick(ax, az, r - ay)
                    for k, part in enumerate((ax, ay, az)):
                        if part:
                            weight = influence(square) * part**4 / math.sqrt(square) ** 3
                            energy[k] = energy[k] + weight * total
            alive = vol_ext[r, at : at + SUB, :] > 0
            for k in range(3):
                safe = jnp.where(alive, energy[k], 1.0)
                put(3 + k, y, at, jnp.where(alive, bulk / safe, 1.0))
        return carry

    lax.fori_loop(0, ext.shape[1], factor_row, 0)

    def factor_out(y, carry):
        for k in range(3):
            fac_out[k, y, :, :] = ext[(3 + k) * 5 + 2, y + HORIZON, left : left + cols, :]
        return carry

    lax.fori_loop(0, rows, factor_out, 0)

    for side, delta in enumerate(SIDES):
        arrived(disp_copy, (delta, 0))
    for side, at in ((0, left - HORIZON), (1, right)):

        def edge_row(y, carry):
            for k in range(3):
                value = got_x[side, pl.ds((k * rows + y) * HORIZON, HORIZON), :]
                put(k, y + HORIZON, at, position(k, value, y + HORIZON, at))
            return carry

        lax.fori_loop(0, rows, edge_row, 0)

    def halo_rows(side):
        delta = SIDES[side]
        for dx in (-1, 0, 1):
            arrived(disp_copy, (dx, delta))
        base = 0 if side == 0 else HORIZON + rows

        def halo_row(y, carry):
            row = y + base
            for k in range(3):
                for at in range(0, cols, SUB):
                    value = got_y[side, k, y, at : at + SUB, :]
                    put(k, row, left + at, position(k, value, row, left + at))
                for dx, at in ((-1, left - HORIZON), (1, right)):
                    corner = CORNERS.index((dx, delta))
                    value = got_c[corner, pl.ds((k * HORIZON + y) * HORIZON, HORIZON), :]
                    put(k, row, at, position(k, value, row, at))
            return carry

        lax.fori_loop(0, HORIZON, halo_row, 0)

    kinds = bond_types()

    def force_tile(y, tile):
        at = pl.multiple_of(tile * SUB, SUB)
        row = y + HORIZON

        def load(field, bond):
            ox, oy, oz = bond
            if abs(oz) <= 2:
                return ext[field * 5 + oz + 2, row + oy, pl.ds(at + (left + ox), SUB), :]
            value = shifted(own[field], oz)
            if field == 2:
                value = value + float(oz)
            if field == 6:
                inside = lane < LANES - oz if oz > 0 else lane >= -oz
                value = jnp.where(inside, value, 0.0)
            return value

        own = [ext[f * 5 + 2, row, pl.ds(at + left, SUB), :] for f in range(7)]
        force = [zero, zero, zero]
        for kind, bonds in kinds.items():
            square = sum(a * a for a in kind)
            length = math.sqrt(square)
            common = math.gcd(*kind)
            count = sum(a > 0 for a in kind)
            scale = 0.5 if count == 1 else length / (2.0 * common)
            scale = STIFF * influence(square) * scale
            total = [zero, zero, zero]
            for bond in bonds:
                apart = [load(k, bond) - own[k] for k in range(3)]
                squared = apart[0] * apart[0] + apart[1] * apart[1] + apart[2] * apart[2]
                pull = 1.0 / length - lax.rsqrt(squared)
                near = [k for k in range(3) if bond[k]]
                pair = {k: own[3 + k] + load(3 + k, bond) for k in near}
                if count == 1:
                    ratio = pair[near[0]]
                else:
                    two = {k: pair[k] * pair[k] for k in near}
                    part = {k: (bond[k] // common) ** 2 for k in near}
                    if count == 2:
                        a, b = near
                        left_term = two[b] if part[a] == 1 else two[b] * float(part[a])
                        right_term = two[a] if part[b] == 1 else two[a] * float(part[b])
                        ratio = pair[a] * pair[b] * lax.rsqrt(left_term + right_term)
                    else:
                        odd = next(
                            k for k in near if sum(part[j] == part[k] for j in near) in (1, 3)
                        )
                        a, b = [k for k in near if k != odd]
                        first = two[a] * two[b]
                        if part[odd] != 1:
                            first = first * float(part[odd])
                        second = two[odd] * (two[a] + two[b])
                        if part[a] != 1:
                            second = second * float(part[a])
                        ratio = pair[a] * pair[b] * pair[odd] * lax.rsqrt(first + second)
                factor = (ratio * pull) * load(6, bond)
                total = [total[k] + factor * apart[k] for k in range(3)]
            force = [force[k] + scale * total[k] for k in range(3)]
        alive = own[6] > 0
        for k in range(3):
            force_out[k, y, pl.ds(at, SUB), :] = jnp.where(alive, force[k], 0.0)

    def force_row(i, carry):
        y = lax.rem(i + HORIZON, rows)

        @pl.when(i == rows - 2 * HORIZON)
        def _():
            halo_rows(1)

        @pl.when(i == rows - HORIZON)
        def _():
            halo_rows(0)

        def one(tile, inner):
            force_tile(y, tile)
            return inner

        return lax.fori_loop(0, cols // SUB, one, carry)

    lax.fori_loop(0, rows, force_row, 0)

    for make in (vol_copy, disp_copy):
        for step in order:

            @pl.when(has(step))
            def _():
                make(step).wait_send()


def shards(displacement, volume, material, layers):
    _, rows, cols, depth = displacement.shape
    wide_rows, wide_cols = rows + 2 * WIDE, cols + 2 * SUB
    near_rows = rows + 2 * HORIZON
    near_tiles = -(-(cols + 2 * HORIZON) // SUB)
    vmem = pl.BlockSpec(memory_space=pltpu.VMEM)
    edge = -(-3 * rows * HORIZON // SUB) * SUB
    corner = -(-3 * HORIZON * HORIZON // SUB) * SUB
    result = jax.ShapeDtypeStruct((3, rows, cols, depth), jnp.float32)

    def scratch(*shape):
        return pltpu.VMEM(shape + (depth,), jnp.float32)

    return pl.pallas_call(
        kernel,
        out_shape=(result, result),
        in_specs=[vmem] * 4,
        out_specs=(vmem, vmem),
        scratch_shapes=[
            scratch(wide_rows, wide_cols),
            scratch(HORIZON, wide_rows, wide_cols),
            scratch(len(TPAIRS), wide_rows, near_tiles * SUB),
            scratch(35, near_rows, wide_cols),
            scratch(2, edge),
            scratch(4, corner),
            scratch(2, 3, HORIZON, cols),
            scratch(2, edge),
            scratch(4, corner),
            pltpu.SemaphoreType.DMA((4, len(STEPS))),
        ],
        compiler_params=pltpu.CompilerParams(collective_id=0, has_side_effects=True),
        name="bonds",
    )(displacement, volume, material, layers)


def solution(mesh):
    return jax.shard_map(
        shards,
        mesh=mesh,
        in_specs=(P(None, "gy", "gx", None), P("gy", "gx", None), P("gy", "gx"), P("gy", "gx")),
        out_specs=(P(None, "gy", "gx", None), P(None, "gy", "gx", None)),
        check_vma=False,
    )
```

profile of v0, /device:TPU:27, one launch (start us, length us, event | category | flops | bytes accessed | tf_op | source)
XLA Modules:
  0.0 46.3 jit_solution(8457241157253859416)
XLA Ops:
  0.6 43.0 %bonds.1 = (f32[3,8,32,128]{3,2,1,0:T(8,128)}, f32[3,8,32,128]{3,2,1,0:T(8,128)}) custom-call(f32[3,8,32,128]{3,2,1,0:T(8,128)} %disp.1, f32[8,32,128]{2,1,0:T(8,128)} %volume.1, s32[8,32]{1,0:T(8,128)} %material.1, s32[8,32]{1,0:T(8,128)} %layers.1), custom_call_target="tpu_custom_call" | custom-call | tf_op jit(solution)/shard_map/bonds/pallas_call | solution.py:437
  43.7 0.0 copy-start
  43.7 1.8 %copy.8 = f32[3,8,32,128]{3,2,1,0:T(8,128)} copy(f32[3,8,32,128]{3,2,1,0:T(8,128)} %get-tuple-element.4) | data formatting | bytes 786432
  45.5 0.0 copy-done
  45.5 0.7 %copy.9 = f32[3,8,32,128]{3,2,1,0:T(8,128)} copy(f32[3,8,32,128]{3,2,1,0:T(8,128)S(1)} %copy-done) | data formatting | bytes 786432
Async XLA Ops:
  43.7 1.8 %copy-start = (f32[3,8,32,128]{3,2,1,0:T(8,128)S(1)}, f32[3,8,32,128]{3,2,1,0:T(8,128)}, u32[]{:S(2)}) copy-start(f32[3,8,32,128]{3,2,1,0:T(8,128)} %get-tuple-element.5) | copy-start | bytes 1179652
where the time goes:
time: 47.1 us; the launch traced here: 46.3 us
  Pallas kernels  43 us (91%)
  local copies, waits for them, and re-layouts  2.57 us (5%)
  between operations  0.65 us (1%)
    pallas_call x1, Pallas kernels, shards(): pl.pallas_call(kernel, out_shape=(result, result), in_specs=[vmem] * 4, o...  43 us
    unnamed x4, local copies, waits for them, and re-layouts  2.57 us

commit v1 on v0

v1 whole, which is shorter than its diff:
```python
import math

import jax
import jax.numpy as jnp
from jax import lax
from jax.experimental import pallas as pl
from jax.experimental.pallas import tpu as pltpu
from jax.sharding import PartitionSpec as P

HORIZON = 3
STIFF = 5.0
WIDE = 2 * HORIZON
LANES = 128
SUB = 8
MESH = pl.DeviceIdType.MESH
SIDES = (-1, 1)
STEPS = tuple((dx, dy) for dy in (-1, 0, 1) for dx in (-1, 0, 1) if (dx, dy) != (0, 0))
CORNERS = tuple(step for step in STEPS if step[0] and step[1])


def bond_list():
    reach = range(-HORIZON, HORIZON + 1)
    return [
        (x, y, z)
        for y in reach
        for x in reach
        for z in reach
        if 0 < x * x + y * y + z * z <= HORIZON * HORIZON
    ]


def bond_types(oz):
    kinds = {}
    for bond in bond_list():
        if bond[2] == oz:
            kinds.setdefault(tuple(sorted(map(abs, bond))), []).append(bond)
    return kinds


def influence(square):
    return (1.0 - square / (HORIZON * HORIZON)) ** 2


def moved(value, step):
    return pltpu.roll(value, (-step) % LANES, 1) if step else value


def kernel(
    disp_in, volume_in, material_in, layers_in, fac_out, force_out,
    disp, volume, material, layers, vol_ext, ext, force_buf,
    send_xv, send_cv, send_x, send_c, got_xv, got_cv, got_y, got_x, got_c,
    sems, load_sems, out_sems, fac_sem,
):
    rows, cols = volume.shape[0], volume.shape[1]
    left = SUB
    right = left + cols
    bottom = WIDE + rows
    gx, gy = lax.axis_index("gx"), lax.axis_index("gy")
    nx, ny = lax.axis_size("gx"), lax.axis_size("gy")

    def has(step):
        dx, dy = step
        found = None
        for delta, at, size in ((dx, gx, nx), (dy, gy, ny)):
            if delta:
                test = at > 0 if delta < 0 else at < size - 1
                found = test if found is None else found & test
        return found

    def device(step):
        return {"gx": gx + step[0], "gy": gy + step[1]}

    barrier = pltpu.get_barrier_semaphore()
    for step in STEPS:

        @pl.when(has(step))
        def _():
            pl.semaphore_signal(barrier, inc=1, device_id=device(step), device_id_type=MESH)

    loads = [
        pltpu.make_async_copy(source, target, load_sems.at[index])
        for index, (source, target) in enumerate(
            ((material_in, material), (layers_in, layers), (volume_in, volume), (disp_in, disp))
        )
    ]
    for copy in loads:
        copy.start()

    lane = lax.broadcasted_iota(jnp.int32, (SUB, LANES), 1)
    sub_f = lax.broadcasted_iota(jnp.int32, (SUB, LANES), 0).astype(jnp.float32)
    zero = jnp.zeros((SUB, LANES), jnp.float32)

    def clear(ref, *where):
        ref[where] = jnp.zeros(ref.at[where].shape, jnp.float32)

    @pl.when(gy == 0)
    def _():
        clear(vol_ext, slice(0, WIDE), slice(left, right))
        clear(got_y, 0)

    @pl.when(gy == ny - 1)
    def _():
        clear(vol_ext, slice(bottom, bottom + WIDE), slice(left, right))
        clear(got_y, 1)

    for side, delta in enumerate(SIDES):

        @pl.when(jnp.logical_not(has((delta, 0))))
        def _():
            clear(got_xv, side)
            clear(got_x, side)

    for index, step in enumerate(CORNERS):

        @pl.when(jnp.logical_not(has(step)))
        def _():
            clear(got_cv, index)
            clear(got_c, index)

    for copy in loads[:3]:
        copy.wait()
    eye_row = lax.broadcasted_iota(jnp.int32, (cols, cols), 0)
    eye_col = lax.broadcasted_iota(jnp.int32, (cols, cols), 1)
    level = lax.broadcasted_iota(jnp.int32, (cols, LANES), 1).astype(jnp.float32)
    filled = jnp.where(material[...] > 0, layers[...], 0).astype(jnp.float32)
    for y in range(rows):
        line = jnp.broadcast_to(filled[y : y + 1, :], (cols, cols))
        top = jnp.sum(jnp.where(eye_row == eye_col, line, 0.0), axis=1, keepdims=True)
        vol_ext[WIDE + y, left:right, :] = jnp.where(
            level < jnp.broadcast_to(top, (cols, LANES)), volume[y], 0.0
        )

    loads[3].wait()
    for side, delta in enumerate(SIDES):
        first = left if delta < 0 else right - WIDE
        for y in range(rows):
            send_xv[side, y * WIDE : (y + 1) * WIDE, :] = vol_ext[WIDE + y, first : first + WIDE, :]
        first = 0 if delta < 0 else cols - HORIZON
        for k in range(3):
            for y in range(rows):
                at = (k * rows + y) * HORIZON
                send_x[side, at : at + HORIZON, :] = disp[k, y, first : first + HORIZON, :]
    for index, (dx, dy) in enumerate(CORNERS):
        first = left if dx < 0 else right - WIDE
        start = WIDE if dy < 0 else bottom - WIDE
        for y in range(WIDE):
            at = y * WIDE
            send_cv[index, at : at + WIDE, :] = vol_ext[start + y, first : first + WIDE, :]
        first = 0 if dx < 0 else cols - HORIZON
        start = 0 if dy < 0 else rows - HORIZON
        for k in range(3):
            for y in range(HORIZON):
                at = (k * HORIZON + y) * HORIZON
                send_c[index, at : at + HORIZON, :] = disp[k, start + y, first : first + HORIZON, :]

    middle_x = left + cols // 2
    middle_y = HORIZON + rows // 2

    def place(k, value, y, at):
        width = value.shape[0]
        if k == 0:
            value = value + (sub_f[:width] + float(at - middle_x))
        if k == 1:
            value = value + (y - middle_y).astype(jnp.float32)
        ext[k, y, at : at + width, :] = value

    def own_row(y, carry):
        for k in range(3):
            for at in range(0, cols, SUB):
                place(k, disp[k, y, at : at + SUB, :], y + HORIZON, left + at)
        return carry

    lax.fori_loop(0, rows, own_row, 0)

    peers = sum(has(step).astype(jnp.int32) for step in STEPS)
    pl.semaphore_wait(barrier, peers)

    def cut_from(delta, size, width):
        return {-1: (0, width), 0: (0, size), 1: (size - width, width)}[delta]

    def vol_copy(step):
        dx, dy = step
        if dx == 0:
            y0 = WIDE if dy < 0 else bottom - WIDE
            to_y = bottom if dy < 0 else 0
            source = vol_ext.at[y0 : y0 + WIDE, left:right]
            target = vol_ext.at[to_y : to_y + WIDE, left:right]
        elif dy == 0:
            source, target = send_xv.at[0 if dx < 0 else 1], got_xv.at[0 if dx > 0 else 1]
        else:
            source, target = send_cv.at[CORNERS.index(step)], got_cv.at[CORNERS.index((-dx, -dy))]
        return pltpu.make_async_remote_copy(
            src_ref=source,
            dst_ref=target,
            send_sem=sems.at[0, STEPS.index(step)],
            recv_sem=sems.at[1, STEPS.index((-dx, -dy))],
            device_id=device(step),
            device_id_type=MESH,
        )

    def disp_copy(step):
        dx, dy = step
        if dx == 0:
            y0, yn = cut_from(dy, rows, HORIZON)
            source, target = disp.at[:, y0 : y0 + yn], got_y.at[0 if dy > 0 else 1]
        elif dy == 0:
            source, target = send_x.at[0 if dx < 0 else 1], got_x.at[0 if dx > 0 else 1]
        else:
            source, target = send_c.at[CORNERS.index(step)], got_c.at[CORNERS.index((-dx, -dy))]
        return pltpu.make_async_remote_copy(
            src_ref=source,
            dst_ref=target,
            send_sem=sems.at[2, STEPS.index(step)],
            recv_sem=sems.at[3, STEPS.index((-dx, -dy))],
            device_id=device(step),
            device_id_type=MESH,
        )

    order = sorted(STEPS, key=lambda step: (-abs(step[0]) - abs(step[1]), -abs(step[0])))
    for make in (vol_copy, disp_copy):
        for step in order:

            @pl.when(has(step))
            def _():
                make(step).start()

    def arrived(make, step):
        @pl.when(has(step))
        def _():
            dx, dy = step
            make((-dx, -dy)).wait_recv()

    for step in order:
        arrived(vol_copy, step)
    for side in range(2):
        first = left - WIDE if side == 0 else right
        for y in range(rows):
            at = y * WIDE
            vol_ext[WIDE + y, first : first + WIDE, :] = got_xv[side, at : at + WIDE, :]
    for index, (dx, dy) in enumerate(CORNERS):
        first = left - WIDE if dx < 0 else right
        start = 0 if dy < 0 else bottom
        for y in range(WIDE):
            at = y * WIDE
            vol_ext[start + y, first : first + WIDE, :] = got_cv[index, at : at + WIDE, :]

    bulk = math.pi * HORIZON**4 / 30.0
    near_rows = ext.shape[1]
    near_tiles = -(-(cols + 2 * HORIZON) // SUB)

    def inside(step):
        return lane < LANES - step if step > 0 else lane >= -step

    def factor_tile(y, at):
        row = y + HORIZON
        beside = {}
        for ax in range(HORIZON + 1):
            for ay in range(HORIZON + 1):
                if ax * ax + ay * ay > HORIZON * HORIZON:
                    continue
                total = None
                for dy in sorted({ay, -ay}):
                    for dx in sorted({ax, -ax}):
                        term = vol_ext[row + dy, at + dx : at + dx + SUB, :]
                        total = term if total is None else total + term
                beside[ax, ay] = total
        energy = [None, None, None]
        for k in range(3):
            for az in range(HORIZON + 1):
                layer = None
                for (ax, ay), total in beside.items():
                    square = ax * ax + ay * ay + az * az
                    part = (ax, ay, az)[k]
                    if not 0 < square <= HORIZON * HORIZON or not part:
                        continue
                    term = (influence(square) * part**4 / math.sqrt(square) ** 3) * total
                    layer = term if layer is None else layer + term
                if layer is None:
                    continue
                if az:
                    ahead = jnp.where(inside(az), moved(layer, az), 0.0)
                    layer = ahead + jnp.where(inside(-az), moved(layer, -az), 0.0)
                energy[k] = layer if energy[k] is None else energy[k] + layer
        alive = vol_ext[row, at : at + SUB, :] > 0
        for k in range(3):
            safe = jnp.where(alive, energy[k], 1.0)
            ext[3 + k, y, at : at + SUB, :] = jnp.where(alive, bulk / safe, 1.0)

    def factor_rows(i, carry):
        for y in range(2):
            for tile in range(near_tiles):
                factor_tile(i * 2 + y, left - HORIZON + tile * SUB)
        return carry

    lax.fori_loop(0, near_rows // 2, factor_rows, 0)
    own_rows = slice(HORIZON, HORIZON + rows)
    fac_copy = pltpu.make_async_copy(ext.at[3:6, own_rows, left:right], fac_out, fac_sem)
    fac_copy.start()

    for side, delta in enumerate(SIDES):
        arrived(disp_copy, (delta, 0))
    for side, at in ((0, left - HORIZON), (1, right)):

        def edge_row(y, carry):
            for k in range(3):
                value = got_x[side, pl.ds((k * rows + y) * HORIZON, HORIZON), :]
                place(k, value, y + HORIZON, at)
            return carry

        lax.fori_loop(0, rows, edge_row, 0)

    def halo_rows(side):
        delta = SIDES[side]
        for dx in (-1, 0, 1):
            arrived(disp_copy, (dx, delta))
        base = 0 if side == 0 else HORIZON + rows

        def halo_row(y, carry):
            row = y + base
            for k in range(3):
                for at in range(0, cols, SUB):
                    place(k, got_y[side, k, y, at : at + SUB, :], row, left + at)
                for dx, at in ((-1, left - HORIZON), (1, right)):
                    corner = CORNERS.index((dx, delta))
                    value = got_c[corner, pl.ds((k * HORIZON + y) * HORIZON, HORIZON), :]
                    place(k, value, row, at)
            return carry

        lax.fori_loop(0, HORIZON, halo_row, 0)

    def force_tile(y, tile):
        start = pl.multiple_of(tile * SUB, SUB)
        row = y + HORIZON

        def load(field, ox, oy):
            at = pl.ds(start + (left + ox), SUB)
            if field == 6:
                return vol_ext[row + HORIZON + oy, at, :]
            return ext[field, row + oy, at, :]

        own = [load(f, 0, 0) for f in range(6)]
        force = [None, None, None]
        for oz in sorted(range(-HORIZON, HORIZON + 1), key=abs):
            kinds = bond_types(oz)
            mine = [moved(value, -oz) for value in own]
            if oz:
                mine[2] = mine[2] - float(oz)
            summed = [None, None, None]

            def add(sums, factor, values):
                for k in range(3):
                    term = factor * values[k]
                    sums[k] = term if sums[k] is None else sums[k] + term

            for kind, bonds in kinds.items():
                square = sum(a * a for a in kind)
                length = math.sqrt(square)
                common = math.gcd(*kind)
                count = sum(a > 0 for a in kind)
                scale = 0.5 if count == 1 else length / (2.0 * common)
                scale = STIFF * influence(square) * scale
                late = len(bonds) > 6
                total = [None, None, None]
                for bond in bonds:
                    ox, oy, _ = bond
                    apart = [load(k, ox, oy) - mine[k] for k in range(3)]
                    squared = apart[0] * apart[0] + apart[1] * apart[1] + apart[2] * apart[2]
                    if late:
                        pull = 1.0 / length - lax.rsqrt(squared)
                    else:
                        pull = scale / length - scale * lax.rsqrt(squared)
                    near = [k for k in range(3) if bond[k]]
                    pair = {k: mine[3 + k] + load(3 + k, ox, oy) for k in near}
                    if count == 1:
                        ratio = pair[near[0]]
                    else:
                        two = {k: pair[k] * pair[k] for k in near}
                        part = {k: (bond[k] // common) ** 2 for k in near}
                        if count == 2:
                            a, b = near
                            first = two[b] if part[a] == 1 else two[b] * float(part[a])
                            second = two[a] if part[b] == 1 else two[a] * float(part[b])
                            ratio = pair[a] * pair[b] * lax.rsqrt(first + second)
                        else:
                            odd = next(
                                k for k in near if sum(part[j] == part[k] for j in near) in (1, 3)
                            )
                            a, b = [k for k in near if k != odd]
                            first = two[a] * two[b]
                            if part[odd] != 1:
                                first = first * float(part[odd])
                            second = two[odd] * (two[a] + two[b])
                            if part[a] != 1:
                                second = second * float(part[a])
                            ratio = pair[a] * pair[b] * pair[odd] * lax.rsqrt(first + second)
                    factor = (ratio * pull) * load(6, ox, oy)
                    add(total if late else summed, factor, apart)
                if late:
                    add(summed, scale, total)
            if oz:
                summed = [jnp.where(inside(oz), moved(value, oz), 0.0) for value in summed]
                force = [force[k] + summed[k] for k in range(3)]
            else:
                force = summed
        alive = load(6, 0, 0) > 0
        for k in range(3):
            force_buf[k, y, pl.ds(start, SUB), :] = jnp.where(alive, force[k], 0.0)

    def out_copy(y):
        return pltpu.make_async_copy(force_buf.at[:, y], force_out.at[:, y], out_sems.at[y])

    def force_row(i, carry):
        y = lax.rem(i + HORIZON, rows)

        @pl.when(i == rows - 2 * HORIZON)
        def _():
            halo_rows(1)

        @pl.when(i == rows - HORIZON)
        def _():
            halo_rows(0)

        def one(tile, inner):
            force_tile(y, tile)
            return inner

        lax.fori_loop(0, cols // SUB, one, 0)
        out_copy(y).start()
        return carry

    lax.fori_loop(0, rows, force_row, 0)

    for make in (vol_copy, disp_copy):
        for step in order:

            @pl.when(has(step))
            def _():
                make(step).wait_send()

    fac_copy.wait()
    for y in range(rows):
        out_copy(y).wait()


def shards(displacement, volume, material, layers):
    _, rows, cols, depth = displacement.shape
    wide_rows, wide_cols = rows + 2 * WIDE, cols + 2 * SUB
    near_rows = rows + 2 * HORIZON
    hbm = pl.BlockSpec(memory_space=pltpu.MemorySpace.HBM)
    result = jax.ShapeDtypeStruct((3, rows, cols, depth), jnp.float32)

    def whole(count):
        return -(-count // SUB) * SUB

    edge, corner = whole(3 * rows * HORIZON), whole(3 * HORIZON * HORIZON)
    edge_vol, corner_vol = whole(rows * WIDE), whole(WIDE * WIDE)

    def scratch(*shape):
        return pltpu.VMEM(shape + (depth,), jnp.float32)

    return pl.pallas_call(
        kernel,
        out_shape=(result, result),
        in_specs=[hbm] * 4,
        out_specs=(hbm, hbm),
        scratch_shapes=[
            scratch(3, rows, cols),
            scratch(rows, cols),
            pltpu.VMEM((rows, cols), jnp.int32),
            pltpu.VMEM((rows, cols), jnp.int32),
            scratch(wide_rows, wide_cols),
            scratch(6, near_rows, wide_cols),
            scratch(3, rows, cols),
            scratch(2, edge_vol),
            scratch(4, corner_vol),
            scratch(2, edge),
            scratch(4, corner),
            scratch(2, edge_vol),
            scratch(4, corner_vol),
            scratch(2, 3, HORIZON, cols),
            scratch(2, edge),
            scratch(4, corner),
            pltpu.SemaphoreType.DMA((4, len(STEPS))),
            pltpu.SemaphoreType.DMA((4,)),
            pltpu.SemaphoreType.DMA((rows,)),
            pltpu.SemaphoreType.DMA,
        ],
        compiler_params=pltpu.CompilerParams(collective_id=0, has_side_effects=True),
        name="bonds",
    )(displacement, volume, material, layers)


def solution(mesh):
    return jax.shard_map(
        shards,
        mesh=mesh,
        in_specs=(P(None, "gy", "gx", None), P("gy", "gx", None), P("gy", "gx"), P("gy", "gx")),
        out_specs=(P(None, "gy", "gx", None), P(None, "gy", "gx", None)),
        check_vma=False,
    )
```

time: 47.1 us -> 35.8 us (0.76); the launches traced: 46.3 us -> 35.6 us
  Pallas kernels: 43 us -> 32.4 us
    pallas_call x1, Pallas kernels: 43 us -> 32.4 us  [shards(): pl.pallas_call(kernel, out_shape=(result, result), in_specs=[hbm] * 4, ou...]
where the time goes in v1:
time: 35.8 us; the launch traced here: 35.6 us
  Pallas kernels  32.4 us (91%)
  local copies, waits for them, and re-layouts  2.57 us (7%)
  between operations  0.65 us (2%)
    pallas_call x1, Pallas kernels, shards(): pl.pallas_call(kernel, out_shape=(result, result), in_specs=[hbm] * 4, ou...  32.4 us
    unnamed x4, local copies, waits for them, and re-layouts  2.57 us

profile of v1, /device:TPU:27, one launch (start us, length us, event | category | flops | bytes accessed | tf_op | source)
XLA Modules:
  0.0 35.6 jit_solution(6307282764667956959)
XLA Ops:
  0.6 32.4 %bonds.1 = (f32[3,8,32,128]{3,2,1,0:T(8,128)}, f32[3,8,32,128]{3,2,1,0:T(8,128)}) custom-call(f32[3,8,32,128]{3,2,1,0:T(8,128)} %disp_in.1, f32[8,32,128]{2,1,0:T(8,128)} %volume_in.1, s32[8,32]{1,0:T(8,128)} %material_in.1, s32[8,32]{1,0:T(8,128)} %layers_in.1), custom_call_target="tpu_custom_call" | custom-call | tf_op jit(solution)/shard_map/bonds/pallas_call | solution.py:461
  33.0 0.0 copy-start
  33.0 1.8 %copy.8 = f32[3,8,32,128]{3,2,1,0:T(8,128)} copy(f32[3,8,32,128]{3,2,1,0:T(8,128)} %get-tuple-element.4) | data formatting | bytes 786432
  34.9 0.0 copy-done
  34.9 0.7 %copy.9 = f32[3,8,32,128]{3,2,1,0:T(8,128)} copy(f32[3,8,32,128]{3,2,1,0:T(8,128)S(1)} %copy-done) | data formatting | bytes 786432
Async XLA Ops:
  33.0 1.8 %copy-start = (f32[3,8,32,128]{3,2,1,0:T(8,128)S(1)}, f32[3,8,32,128]{3,2,1,0:T(8,128)}, u32[]{:S(2)}) copy-start(f32[3,8,32,128]{3,2,1,0:T(8,128)} %get-tuple-element.5) | copy-start | bytes 1179652

commit v2 on v1

--- a/solution.py
+++ b/solution.py
@@ -11,6 +11,7 @@
 STIFF = 5.0
 WIDE = 2 * HORIZON
 LANES = 128
+VMEM_LIMIT = 24 * 2**20
 SUB = 8
 MESH = pl.DeviceIdType.MESH
 SIDES = (-1, 1)
@@ -41,15 +42,100 @@
     return (1.0 - square / (HORIZON * HORIZON)) ** 2
 
 
+AWAY = tuple(oz for oz in range(-HORIZON, HORIZON + 1) if oz)
+
+
 def moved(value, step):
     return pltpu.roll(value, (-step) % LANES, 1) if step else value
 
 
+def inside(lane, step):
+    return lane < LANES - step if step > 0 else lane >= -step
+
+
+def middle_row(rows, index):
+    return lax.rem(index + HORIZON, rows)
+
+
+def force_tile(vol_ext, ext, mine, sums, y, slot, tile):
+    start = pl.multiple_of(tile * SUB, SUB)
+    row = y + HORIZON
+
+    def load(field, ox, oy):
+        at = pl.ds(start + (SUB + ox), SUB)
+        if field == 6:
+            return vol_ext[row + HORIZON + oy, at, :]
+        return ext[field, row + oy, at, :]
+
+    for oz in sorted(range(-HORIZON, HORIZON + 1), key=abs):
+        kinds = bond_types(oz)
+        own = {}
+        for f in range(6):
+            if oz == 0:
+                own[f] = load(f, 0, 0)
+            elif f < 3 or f == 5 or abs(oz) < HORIZON:
+                own[f] = mine[f, AWAY.index(oz), y, pl.ds(start + SUB, SUB), :]
+        summed = [None, None, None]
+
+        def add(sums, factor, values):
+            for k in range(3):
+                term = factor * values[k]
+                sums[k] = term if sums[k] is None else sums[k] + term
+
+        for kind, bonds in kinds.items():
+            square = sum(a * a for a in kind)
+            length = math.sqrt(square)
+            common = math.gcd(*kind)
+            count = sum(a > 0 for a in kind)
+            scale = 0.5 if count == 1 else length / (2.0 * common)
+            scale = STIFF * influence(square) * scale
+            late = len(bonds) > 6
+            total = [None, None, None]
+            for bond in bonds:
+                ox, oy, _ = bond
+                apart = [load(k, ox, oy) - own[k] for k in range(3)]
+                squared = apart[0] * apart[0] + apart[1] * apart[1] + apart[2] * apart[2]
+                if late:
+                    pull = 1.0 / length - lax.rsqrt(squared)
+                else:
+                    pull = scale / length - scale * lax.rsqrt(squared)
+                near = [k for k in range(3) if bond[k]]
+                pair = {k: own[3 + k] + load(3 + k, ox, oy) for k in near}
+                if count == 1:
+                    ratio = pair[near[0]]
+                else:
+                    two = {k: pair[k] * pair[k] for k in near}
+                    part = {k: (bond[k] // common) ** 2 for k in near}
+                    if count == 2:
+                        a, b = near
+                        first = two[b] if part[a] == 1 else two[b] * float(part[a])
+                        second = two[a] if part[b] == 1 else two[a] * float(part[b])
+                        ratio = pair[a] * pair[b] * lax.rsqrt(first + second)
+                    else:
+                        odd = next(
+                            k for k in near if sum(part[j] == part[k] for j in near) in (1, 3)
+                        )
+                        a, b = [k for k in near if k != odd]
+                        first = two[a] * two[b]
+                        if part[odd] != 1:
+                            first = first * float(part[odd])
+                        second = two[odd] * (two[a] + two[b])
+                        if part[a] != 1:
+                            second = second * float(part[a])
+                        ratio = pair[a] * pair[b] * pair[odd] * lax.rsqrt(first + second)
+                factor = (ratio * pull) * load(6, ox, oy)
+                add(total if late else summed, factor, apart)
+            if late:
+                add(summed, scale, total)
+        for k in range(3):
+            sums[k, oz + HORIZON, slot, pl.ds(start, SUB), :] = summed[k]
+
+
 def kernel(
-    disp_in, volume_in, material_in, layers_in, fac_out, force_out,
-    disp, volume, material, layers, vol_ext, ext, force_buf,
+    disp_in, volume_in, material_in, layers_in, vol_ext, ext, mine, sums,
+    disp, volume, material, layers,
     send_xv, send_cv, send_x, send_c, got_xv, got_cv, got_y, got_x, got_c,
-    sems, load_sems, out_sems, fac_sem,
+    sems, load_sems,
 ):
     rows, cols = volume.shape[0], volume.shape[1]
     left = SUB
@@ -165,9 +251,15 @@
         ext[k, y, at : at + width, :] = value
 
     def own_row(y, carry):
-        for k in range(3):
-            for at in range(0, cols, SUB):
+        for at in range(0, cols, SUB):
+            for k in range(3):
                 place(k, disp[k, y, at : at + SUB, :], y + HORIZON, left + at)
+                value = ext[k, y + HORIZON, left + at : left + at + SUB, :]
+                for oz in AWAY:
+                    there = moved(value, -oz)
+                    if k == 2:
+                        there = there - float(oz)
+                    mine[k, AWAY.index(oz), y, left + at : left + at + SUB, :] = there
         return carry
 
     lax.fori_loop(0, rows, own_row, 0)
@@ -247,9 +339,6 @@
     bulk = math.pi * HORIZON**4 / 30.0
     near_rows = ext.shape[1]
     near_tiles = -(-(cols + 2 * HORIZON) // SUB)
-
-    def inside(step):
-        return lane < LANES - step if step > 0 else lane >= -step
 
     def factor_tile(y, at):
         row = y + HORIZON
@@ -278,8 +367,8 @@
                 if layer is None:
                     continue
                 if az:
-                    ahead = jnp.where(inside(az), moved(layer, az), 0.0)
-                    layer = ahead + jnp.where(inside(-az), moved(layer, -az), 0.0)
+                    ahead = jnp.where(inside(lane, az), moved(layer, az), 0.0)
+                    layer = ahead + jnp.where(inside(lane, -az), moved(layer, -az), 0.0)
                 energy[k] = layer if energy[k] is None else energy[k] + layer
         alive = vol_ext[row, at : at + SUB, :] > 0
         for k in range(3):
@@ -293,9 +382,19 @@
         return carry
 
     lax.fori_loop(0, near_rows // 2, factor_rows, 0)
-    own_rows = slice(HORIZON, HORIZON + rows)
-    fac_copy = pltpu.make_async_copy(ext.at[3:6, own_rows, left:right], fac_out, fac_sem)
-    fac_copy.start()
+
+    def factor_moved(i, carry):
+        for part in range(4):
+            y = i * 4 + part
+            for at in range(left, right, SUB):
+                for k in range(3):
+                    value = ext[3 + k, y + HORIZON, at : at + SUB, :]
+                    for oz in AWAY:
+                        if k == 2 or abs(oz) < HORIZON:
+                            mine[3 + k, AWAY.index(oz), y, at : at + SUB, :] = moved(value, -oz)
+        return carry
+
+    lax.fori_loop(0, rows // 4, factor_moved, 0)
 
     for side, delta in enumerate(SIDES):
         arrived(disp_copy, (delta, 0))
@@ -328,107 +427,16 @@
 
         lax.fori_loop(0, HORIZON, halo_row, 0)
 
-    def force_tile(y, tile):
-        start = pl.multiple_of(tile * SUB, SUB)
-        row = y + HORIZON
-
-        def load(field, ox, oy):
-            at = pl.ds(start + (left + ox), SUB)
-            if field == 6:
-                return vol_ext[row + HORIZON + oy, at, :]
-            return ext[field, row + oy, at, :]
-
-        own = [load(f, 0, 0) for f in range(6)]
-        force = [None, None, None]
-        for oz in sorted(range(-HORIZON, HORIZON + 1), key=abs):
-            kinds = bond_types(oz)
-            mine = [moved(value, -oz) for value in own]
-            if oz:
-                mine[2] = mine[2] - float(oz)
-            summed = [None, None, None]
-
-            def add(sums, factor, values):
-                for k in range(3):
-                    term = factor * values[k]
-                    sums[k] = term if sums[k] is None else sums[k] + term
-
-            for kind, bonds in kinds.items():
-                square = sum(a * a for a in kind)
-                length = math.sqrt(square)
-                common = math.gcd(*kind)
-                count = sum(a > 0 for a in kind)
-                scale = 0.5 if count == 1 else length / (2.0 * common)
-                scale = STIFF * influence(square) * scale
-                late = len(bonds) > 6
-                total = [None, None, None]
-                for bond in bonds:
-                    ox, oy, _ = bond
-                    apart = [load(k, ox, oy) - mine[k] for k in range(3)]
-                    squared = apart[0] * apart[0] + apart[1] * apart[1] + apart[2] * apart[2]
-                    if late:
-                        pull = 1.0 / length - lax.rsqrt(squared)
-                    else:
-                        pull = scale / length - scale * lax.rsqrt(squared)
-                    near = [k for k in range(3) if bond[k]]
-                    pair = {k: mine[3 + k] + load(3 + k, ox, oy) for k in near}
-                    if count == 1:
-                        ratio = pair[near[0]]
-                    else:
-                        two = {k: pair[k] * pair[k] for k in near}
-                        part = {k: (bond[k] // common) ** 2 for k in near}
-                        if count == 2:
-                            a, b = near
-                            first = two[b] if part[a] == 1 else two[b] * float(part[a])
-                            second = two[a] if part[b] == 1 else two[a] * float(part[b])
-                            ratio = pair[a] * pair[b] * lax.rsqrt(first + second)
-                        else:
-                            odd = next(
-                                k for k in near if sum(part[j] == part[k] for j in near) in (1, 3)
-                            )
-                            a, b = [k for k in near if k != odd]
-                            first = two[a] * two[b]
-                            if part[odd] != 1:
-                                first = first * float(part[odd])
-                            second = two[odd] * (two[a] + two[b])
-                            if part[a] != 1:
-                                second = second * float(part[a])
-                            ratio = pair[a] * pair[b] * pair[odd] * lax.rsqrt(first + second)
-                    factor = (ratio * pull) * load(6, ox, oy)
-                    add(total if late else summed, factor, apart)
-                if late:
-                    add(summed, scale, total)
-            if oz:
-                summed = [jnp.where(inside(oz), moved(value, oz), 0.0) for value in summed]
-                force = [force[k] + summed[k] for k in range(3)]
-            else:
-                force = summed
-        alive = load(6, 0, 0) > 0
-        for k in range(3):
-            force_buf[k, y, pl.ds(start, SUB), :] = jnp.where(alive, force[k], 0.0)
-
-    def out_copy(y):
-        return pltpu.make_async_copy(force_buf.at[:, y], force_out.at[:, y], out_sems.at[y])
-
-    def force_row(i, carry):
-        y = lax.rem(i + HORIZON, rows)
-
-        @pl.when(i == rows - 2 * HORIZON)
-        def _():
-            halo_rows(1)
-
-        @pl.when(i == rows - HORIZON)
-        def _():
-            halo_rows(0)
-
+    def row(i, carry):
         def one(tile, inner):
-            force_tile(y, tile)
+            force_tile(vol_ext, ext, mine, sums, middle_row(rows, i), i, tile)
             return inner
 
-        lax.fori_loop(0, cols // SUB, one, 0)
-        out_copy(y).start()
-        return carry
-
-    lax.fori_loop(0, rows, force_row, 0)
+        return lax.fori_loop(0, cols // SUB, one, carry)
+
+    lax.fori_loop(0, rows - 2 * HORIZON, row, 0)
+    for side in (1, 0):
+        halo_rows(side)
 
     for make in (vol_copy, disp_copy):
         for step in order:
@@ -437,6 +445,50 @@
             def _():
                 make(step).wait_send()
 
+
+def rest(
+    vol_ext, ext, mine, early, fac_out, force_out, sums, force, out_sems, fac_sem
+):
+    rows, cols = force.shape[1], force.shape[2]
+    lane = lax.broadcasted_iota(jnp.int32, (SUB, LANES), 1)
+    own = ext.at[3:6, HORIZON : HORIZON + rows, SUB : SUB + cols]
+    fac_copy = pltpu.make_async_copy(own, fac_out, fac_sem)
+    fac_copy.start()
+    done = early.shape[2]
+    half = sums.shape[2]
+
+    def out_copy(y):
+        return pltpu.make_async_copy(force.at[:, y], force_out.at[:, y], out_sems.at[y])
+
+    def finish(parts, slot, y):
+        for at in range(0, cols, SUB):
+            alive = vol_ext[y + WIDE, SUB + at : 2 * SUB + at, :] > 0
+            for k in range(3):
+                total = parts[k, HORIZON, slot, at : at + SUB, :]
+                for oz in AWAY:
+                    part = moved(parts[k, oz + HORIZON, slot, at : at + SUB, :], oz)
+                    total = total + jnp.where(inside(lane, oz), part, 0.0)
+                force[k, y, at : at + SUB, :] = jnp.where(alive, total, 0.0)
+        out_copy(y).start()
+
+    def group(first, carry):
+        def row(slot, inner):
+            y = middle_row(rows, first * half + slot + done)
+
+            def one(tile, last):
+                force_tile(vol_ext, ext, mine, sums, y, slot, tile)
+                return last
+
+            return lax.fori_loop(0, cols // SUB, one, inner)
+
+        lax.fori_loop(0, half, row, 0)
+        for slot in range(half):
+            finish(sums, slot, middle_row(rows, first * half + slot + done))
+        return carry
+
+    for slot in range(done):
+        finish(early, slot, (slot + HORIZON) % rows)
+    lax.fori_loop(0, (rows - done) // half, group, 0)
     fac_copy.wait()
     for y in range(rows):
         out_copy(y).wait()
@@ -458,19 +510,30 @@
     def scratch(*shape):
         return pltpu.VMEM(shape + (depth,), jnp.float32)
 
-    return pl.pallas_call(
+    def held(*shape):
+        return pltpu.VMEM(shape + (depth,), jnp.float32)
+
+    def pin(values, space):
+        return [pltpu.with_memory_space_constraint(value, space) for value in values]
+
+    vmem = pl.BlockSpec(memory_space=pltpu.VMEM)
+    early = rows - 2 * HORIZON
+    frames = 2 * HORIZON + 1
+    state = pl.pallas_call(
         kernel,
-        out_shape=(result, result),
+        out_shape=(
+            held(wide_rows, wide_cols),
+            held(6, near_rows, wide_cols),
+            held(6, len(AWAY), rows, wide_cols),
+            held(3, frames, early, cols),
+        ),
         in_specs=[hbm] * 4,
-        out_specs=(hbm, hbm),
+        out_specs=(vmem,) * 4,
         scratch_shapes=[
             scratch(3, rows, cols),
             scratch(rows, cols),
             pltpu.VMEM((rows, cols), jnp.int32),
             pltpu.VMEM((rows, cols), jnp.int32),
-            scratch(wide_rows, wide_cols),
-            scratch(6, near_rows, wide_cols),
-            scratch(3, rows, cols),
             scratch(2, edge_vol),
             scratch(4, corner_vol),
             scratch(2, edge),
@@ -482,12 +545,26 @@
             scratch(4, corner),
             pltpu.SemaphoreType.DMA((4, len(STEPS))),
             pltpu.SemaphoreType.DMA((4,)),
+        ],
+        compiler_params=pltpu.CompilerParams(
+            collective_id=0, has_side_effects=True, vmem_limit_bytes=VMEM_LIMIT
+        ),
+        name="gather",
+    )(*pin((displacement, volume, material, layers), pltpu.MemorySpace.HBM))
+    return pl.pallas_call(
+        rest,
+        out_shape=(result, result),
+        in_specs=[vmem] * 4,
+        out_specs=(hbm, hbm),
+        scratch_shapes=[
+            scratch(3, frames, HORIZON, cols),
+            scratch(3, rows, cols),
             pltpu.SemaphoreType.DMA((rows,)),
             pltpu.SemaphoreType.DMA,
         ],
-        compiler_params=pltpu.CompilerParams(collective_id=0, has_side_effects=True),
-        name="bonds",
-    )(displacement, volume, material, layers)
+        compiler_params=pltpu.CompilerParams(vmem_limit_bytes=VMEM_LIMIT),
+        name="rest",
+    )(*pin(state, pltpu.MemorySpace.VMEM))
 
 
 def solution(mesh):

time: 35.8 us -> 32.1 us (0.90); the launches traced: 35.6 us -> 31.5 us
  local copies, waits for them, and re-layouts: 2.57 us -> 0 us
  Pallas kernels: 32.4 us -> 30.9 us
    unnamed x4 -> x0, local copies, waits for them, and re-layouts: 2.57 us -> none
    pallas_call x1 -> x2, Pallas kernels: 32.4 us -> 30.9 us  [the longest x1 17.6 us: shards(): pl.pallas_call(kernel, out_shape=(held(wide_rows, wide_cols), held(6, nea...]
where the time goes in v2:
time: 32.1 us; the launch traced here: 31.5 us
  Pallas kernels  30.9 us (96%)
  between operations  0.64 us (2%)
    pallas_call x1, Pallas kernels, shards(): pl.pallas_call(kernel, out_shape=(held(wide_rows, wide_cols), held(6, nea...  17.6 us
    pallas_call x1, Pallas kernels, shards(): pl.pallas_call(rest, out_shape=(result, result), in_specs=[vmem] * 4, out...  13.3 us

profile of v2, /device:TPU:27, one launch (start us, length us, event | category | flops | bytes accessed | tf_op | source)
XLA Modules:
  0.0 31.5 jit_solution(13944948861645006602)
XLA Ops:
  0.6 17.6 %gather.1 = (f32[20,48,128]{2,1,0:T(8,128)S(1)}, f32[6,14,48,128]{3,2,1,0:T(8,128)S(1)}, f32[6,6,8,48,128]{4,3,2,1,0:T(8,128)S(1)}, f32[3,7,2,32,128]{4,3,2,1,0:T(8,128)S(1)}) custom-call(f32[3,8,32,128]{3,2,1,0:T(8,128)} %disp_in.1, f32[8,32,128]{2,1,0:T(8,128)} %volume_in.1, s32[8,32]{1,0:T(8,128)} %material_in.1, s32[8,32]{1,0:T(8,128)} %layers_in.1), custom_call_target="tpu_custom_call" | custom-call | tf_op jit(solution)/shard_map/gather/pallas_call | solution.py:522
  18.2 13.3 %rest.1 = (f32[3,8,32,128]{3,2,1,0:T(8,128)}, f32[3,8,32,128]{3,2,1,0:T(8,128)}) custom-call(f32[20,48,128]{2,1,0:T(8,128)S(1)} %get-tuple-element.6.vol_ext, f32[6,14,48,128]{3,2,1,0:T(8,128)S(1)} %get-tuple-element.7.ext, f32[6,6,8,48,128]{4,3,2,1,0:T(8,128)S(1)} %get-tuple-element.8.mine, f32[3,7,2,32,128]{4,3,2,1,0:T(8,128)S(1)} %get-tuple-element.9.early), custom_call_target="tpu_custom_call" | custom-call | tf_op jit(solution)/shard_map/rest/pallas_call | solution.py:554

commit v3 on v2

--- a/solution.py
+++ b/solution.py
@@ -134,8 +134,8 @@
 def kernel(
     disp_in, volume_in, material_in, layers_in, vol_ext, ext, mine, sums,
     disp, volume, material, layers,
-    send_xv, send_cv, send_x, send_c, got_xv, got_cv, got_y, got_x, got_c,
-    sems, load_sems,
+    send_xv, send_cn, send_cf, send_x, send_c, got_xv, got_cn, got_cf, got_y, got_x, got_c,
+    via_xv, via_x, sems, via_sems, load_sems,
 ):
     rows, cols = volume.shape[0], volume.shape[1]
     left = SUB
@@ -153,13 +153,25 @@
                 found = test if found is None else found & test
         return found
 
+    odd = lax.rem(gy, 2)
+    toward = 1 - 2 * odd
+    paired = (gy + toward >= 0) & (gy + toward < ny)
+
+    def to_partner(dy):
+        return odd == (1 if dy < 0 else 0)
+
+    def direct(step):
+        if step in CORNERS:
+            return has(step) & jnp.logical_not(to_partner(step[1]))
+        return has(step)
+
     def device(step):
         return {"gx": gx + step[0], "gy": gy + step[1]}
 
     barrier = pltpu.get_barrier_semaphore()
     for step in STEPS:
 
-        @pl.when(has(step))
+        @pl.when(direct(step))
         def _():
             pl.semaphore_signal(barrier, inc=1, device_id=device(step), device_id_type=MESH)
 
@@ -196,11 +208,17 @@
             clear(got_xv, side)
             clear(got_x, side)
 
+        @pl.when(jnp.logical_not(has((delta, 0)) & paired))
+        def _():
+            clear(via_xv, side)
+            clear(via_x, side)
+
     for index, step in enumerate(CORNERS):
 
         @pl.when(jnp.logical_not(has(step)))
         def _():
-            clear(got_cv, index)
+            clear(got_cn, index)
+            clear(got_cf, index)
             clear(got_c, index)
 
     for copy in loads[:3]:
@@ -216,6 +234,18 @@
             level < jnp.broadcast_to(top, (cols, LANES)), volume[y], 0.0
         )
 
+    def near_row(dy):
+        return WIDE if dy < 0 else bottom - HORIZON
+
+    def far_row(dy):
+        return WIDE + HORIZON if dy < 0 else bottom - WIDE
+
+    def near_halo(dy):
+        return HORIZON if dy < 0 else bottom
+
+    def far_halo(dy):
+        return 0 if dy < 0 else bottom + HORIZON
+
     loads[3].wait()
     for side, delta in enumerate(SIDES):
         first = left if delta < 0 else right - WIDE
@@ -228,10 +258,10 @@
                 send_x[side, at : at + HORIZON, :] = disp[k, y, first : first + HORIZON, :]
     for index, (dx, dy) in enumerate(CORNERS):
         first = left if dx < 0 else right - WIDE
-        start = WIDE if dy < 0 else bottom - WIDE
-        for y in range(WIDE):
-            at = y * WIDE
-            send_cv[index, at : at + WIDE, :] = vol_ext[start + y, first : first + WIDE, :]
+        for buffer, start in ((send_cn, near_row(dy)), (send_cf, far_row(dy))):
+            for y in range(HORIZON):
+                at = y * WIDE
+                buffer[index, at : at + WIDE, :] = vol_ext[start + y, first : first + WIDE, :]
         first = 0 if dx < 0 else cols - HORIZON
         start = 0 if dy < 0 else rows - HORIZON
         for k in range(3):
@@ -264,31 +294,61 @@
 
     lax.fori_loop(0, rows, own_row, 0)
 
-    peers = sum(has(step).astype(jnp.int32) for step in STEPS)
+    peers = sum(direct(step).astype(jnp.int32) for step in STEPS)
     pl.semaphore_wait(barrier, peers)
 
     def cut_from(delta, size, width):
         return {-1: (0, width), 0: (0, size), 1: (size - width, width)}[delta]
 
     def vol_copy(step):
+        return rows_copy(step, near_row, near_halo, send_cn, got_cn, 0)
+
+    def far_copy(step):
+        return rows_copy(step, far_row, far_halo, send_cf, got_cf, 4)
+
+    def rows_copy(step, own, halo, send_corner, got_corner, sem):
         dx, dy = step
         if dx == 0:
-            y0 = WIDE if dy < 0 else bottom - WIDE
-            to_y = bottom if dy < 0 else 0
-            source = vol_ext.at[y0 : y0 + WIDE, left:right]
-            target = vol_ext.at[to_y : to_y + WIDE, left:right]
+            source = vol_ext.at[own(dy) : own(dy) + HORIZON, left:right]
+            target = vol_ext.at[halo(-dy) : halo(-dy) + HORIZON, left:right]
         elif dy == 0:
             source, target = send_xv.at[0 if dx < 0 else 1], got_xv.at[0 if dx > 0 else 1]
         else:
-            source, target = send_cv.at[CORNERS.index(step)], got_cv.at[CORNERS.index((-dx, -dy))]
+            source = send_corner.at[CORNERS.index(step)]
+            target = got_corner.at[CORNERS.index((-dx, -dy))]
         return pltpu.make_async_remote_copy(
             src_ref=source,
             dst_ref=target,
-            send_sem=sems.at[0, STEPS.index(step)],
-            recv_sem=sems.at[1, STEPS.index((-dx, -dy))],
+            send_sem=sems.at[sem, STEPS.index(step)],
+            recv_sem=sems.at[sem + 1, STEPS.index((-dx, -dy))],
             device_id=device(step),
             device_id_type=MESH,
         )
+
+    def via_copy(kind, side):
+        source, target = ((got_xv, via_xv), (got_x, via_x))[kind]
+        return pltpu.make_async_remote_copy(
+            src_ref=source.at[side],
+            dst_ref=target.at[side],
+            send_sem=via_sems.at[2 * kind, side],
+            recv_sem=via_sems.at[2 * kind + 1, side],
+            device_id={"gx": gx, "gy": gy + toward},
+            device_id_type=MESH,
+        )
+
+    def hand_on(kind):
+        for side, delta in enumerate(SIDES):
+
+            @pl.when(has((delta, 0)) & paired)
+            def _():
+                via_copy(kind, side).start()
+
+    def handed(kind):
+        for side, delta in enumerate(SIDES):
+
+            @pl.when(has((delta, 0)) & paired)
+            def _():
+                via_copy(kind, side).wait_recv()
 
     def disp_copy(step):
         dx, dy = step
@@ -308,33 +368,41 @@
             device_id_type=MESH,
         )
 
-    order = sorted(STEPS, key=lambda step: (-abs(step[0]) - abs(step[1]), -abs(step[0])))
-    for make in (vol_copy, disp_copy):
-        for step in order:
-
-            @pl.when(has(step))
-            def _():
-                make(step).start()
+    along_x = [step for step in STEPS if step[1] == 0]
+    along_y = [step for step in STEPS if step[0] == 0]
+    sends = [(vol_copy, step) for step in (*along_y, *along_x, *CORNERS)]
+    sends += [(disp_copy, step) for step in along_x]
+    sends += [(far_copy, step) for step in (*CORNERS, *along_y)]
+    sends += [(disp_copy, step) for step in (*CORNERS, *along_y)]
+    for make, step in sends:
+
+        @pl.when(direct(step))
+        def _():
+            make(step).start()
 
     def arrived(make, step):
-        @pl.when(has(step))
+        @pl.when(direct(step))
         def _():
             dx, dy = step
             make((-dx, -dy)).wait_recv()
 
-    for step in order:
-        arrived(vol_copy, step)
-    for side in range(2):
-        first = left - WIDE if side == 0 else right
-        for y in range(rows):
-            at = y * WIDE
-            vol_ext[WIDE + y, first : first + WIDE, :] = got_xv[side, at : at + WIDE, :]
-    for index, (dx, dy) in enumerate(CORNERS):
-        first = left - WIDE if dx < 0 else right
-        start = 0 if dy < 0 else bottom
-        for y in range(WIDE):
-            at = y * WIDE
-            vol_ext[start + y, first : first + WIDE, :] = got_cv[index, at : at + WIDE, :]
+    def fill_corners(buffer, row_there, row_here):
+        for index, (dx, dy) in enumerate(CORNERS):
+            side = 0 if dx < 0 else 1
+            first = left - WIDE if dx < 0 else right
+            there, here = row_there(-dy) - WIDE, row_here(dy)
+
+            @pl.when(to_partner(dy))
+            def _():
+                for y in range(HORIZON):
+                    at = (there + y) * WIDE
+                    vol_ext[here + y, first : first + WIDE, :] = via_xv[side, at : at + WIDE, :]
+
+            @pl.when(jnp.logical_not(to_partner(dy)))
+            def _():
+                for y in range(HORIZON):
+                    at = y * WIDE
+                    vol_ext[here + y, first : first + WIDE, :] = buffer[index, at : at + WIDE, :]
 
     bulk = math.pi * HORIZON**4 / 30.0
     near_rows = ext.shape[1]
@@ -375,43 +443,71 @@
             safe = jnp.where(alive, energy[k], 1.0)
             ext[3 + k, y, at : at + SUB, :] = jnp.where(alive, bulk / safe, 1.0)
 
-    def factor_rows(i, carry):
-        for y in range(2):
-            for tile in range(near_tiles):
-                factor_tile(i * 2 + y, left - HORIZON + tile * SUB)
-        return carry
-
-    lax.fori_loop(0, near_rows // 2, factor_rows, 0)
-
-    def factor_moved(i, carry):
-        for part in range(4):
-            y = i * 4 + part
-            for at in range(left, right, SUB):
+    def factor_rows(first, step, stride, count, tiles):
+        def body(i, carry):
+            for y in range(count):
+                for tile in tiles:
+                    factor_tile(i * stride + first + y * step, left - HORIZON + tile * SUB)
+            return carry
+
+        return body
+
+    def factor_moved(tiles):
+        def body(i, carry):
+            for part in range(4):
+                y = i * 4 + part
+                for tile in tiles:
+                    at = left + tile * SUB
+                    for k in range(3):
+                        value = ext[3 + k, y + HORIZON, at : at + SUB, :]
+                        for oz in AWAY:
+                            if k == 2 or abs(oz) < HORIZON:
+                                there = moved(value, -oz)
+                                mine[3 + k, AWAY.index(oz), y, at : at + SUB, :] = there
+            return carry
+
+        return body
+
+    def own_factors(near, own):
+        lax.fori_loop(0, rows // 4, factor_rows(HORIZON, 1, 4, 4, near), 0)
+        lax.fori_loop(0, rows // 4, factor_moved(own), 0)
+
+    own_tiles = cols // SUB
+
+    def middle():
+        for step in along_y:
+            arrived(vol_copy, step)
+        own_factors(range(1, near_tiles - 1), range(1, own_tiles - 1))
+
+    def edges():
+        for step in along_x:
+            arrived(vol_copy, step)
+        hand_on(0)
+        for side in range(2):
+            first = left - WIDE if side == 0 else right
+            for y in range(rows):
+                at = y * WIDE
+                vol_ext[WIDE + y, first : first + WIDE, :] = got_xv[side, at : at + WIDE, :]
+        for step in CORNERS:
+            arrived(vol_copy, step)
+        handed(0)
+        fill_corners(got_cn, near_row, near_halo)
+        own_factors((0, near_tiles - 1), (0, own_tiles - 1))
+        for step in along_x:
+            arrived(disp_copy, step)
+        hand_on(1)
+        for side, at in ((0, left - HORIZON), (1, right)):
+
+            def edge_row(y, carry):
                 for k in range(3):
-                    value = ext[3 + k, y + HORIZON, at : at + SUB, :]
-                    for oz in AWAY:
-                        if k == 2 or abs(oz) < HORIZON:
-                            mine[3 + k, AWAY.index(oz), y, at : at + SUB, :] = moved(value, -oz)
-        return carry
-
-    lax.fori_loop(0, rows // 4, factor_moved, 0)
-
-    for side, delta in enumerate(SIDES):
-        arrived(disp_copy, (delta, 0))
-    for side, at in ((0, left - HORIZON), (1, right)):
-
-        def edge_row(y, carry):
-            for k in range(3):
-                value = got_x[side, pl.ds((k * rows + y) * HORIZON, HORIZON), :]
-                place(k, value, y + HORIZON, at)
-            return carry
-
-        lax.fori_loop(0, rows, edge_row, 0)
+                    value = got_x[side, pl.ds((k * rows + y) * HORIZON, HORIZON), :]
+                    place(k, value, y + HORIZON, at)
+                return carry
+
+            lax.fori_loop(0, rows, edge_row, 0)
 
     def halo_rows(side):
         delta = SIDES[side]
-        for dx in (-1, 0, 1):
-            arrived(disp_copy, (dx, delta))
         base = 0 if side == 0 else HORIZON + rows
 
         def halo_row(y, carry):
@@ -421,29 +517,60 @@
                     place(k, got_y[side, k, y, at : at + SUB, :], row, left + at)
                 for dx, at in ((-1, left - HORIZON), (1, right)):
                     corner = CORNERS.index((dx, delta))
-                    value = got_c[corner, pl.ds((k * HORIZON + y) * HORIZON, HORIZON), :]
-                    place(k, value, row, at)
+                    there = y if delta > 0 else y + (rows - HORIZON)
+
+                    @pl.when(to_partner(delta))
+                    def _():
+                        from_via = pl.ds((k * rows + there) * HORIZON, HORIZON)
+                        place(k, via_x[0 if dx < 0 else 1, from_via, :], row, at)
+
+                    @pl.when(jnp.logical_not(to_partner(delta)))
+                    def _():
+                        from_corner = pl.ds((k * HORIZON + y) * HORIZON, HORIZON)
+                        place(k, got_c[corner, from_corner, :], row, at)
+
             return carry
 
         lax.fori_loop(0, HORIZON, halo_row, 0)
 
-    def row(i, carry):
-        def one(tile, inner):
-            force_tile(vol_ext, ext, mine, sums, middle_row(rows, i), i, tile)
-            return inner
-
-        return lax.fori_loop(0, cols // SUB, one, carry)
-
-    lax.fori_loop(0, rows - 2 * HORIZON, row, 0)
+    early = rows - 2 * HORIZON
+    inner = own_tiles - 2
+
+    def tile_step(i, carry):
+        @pl.when(i == early * inner)
+        def _():
+            edges()
+
+        later = i - early * inner
+        slot = jnp.where(later < 0, lax.div(i, inner), lax.div(later, 2))
+        tile = jnp.where(later < 0, lax.rem(i, inner) + 1, lax.rem(later, 2) * (own_tiles - 1))
+        force_tile(vol_ext, ext, mine, sums, middle_row(rows, slot), slot, tile)
+        return carry
+
+    middle()
+    lax.fori_loop(0, early * own_tiles, tile_step, 0)
+    for step in (*CORNERS, *along_y):
+        arrived(far_copy, step)
+    fill_corners(got_cf, far_row, far_halo)
+    lax.fori_loop(0, HORIZON, factor_rows(0, rows + HORIZON, 1, 2, range(near_tiles)), 0)
+    for step in (*CORNERS, *along_y):
+        arrived(disp_copy, step)
+    handed(1)
     for side in (1, 0):
         halo_rows(side)
 
-    for make in (vol_copy, disp_copy):
-        for step in order:
-
-            @pl.when(has(step))
-            def _():
-                make(step).wait_send()
+    for make, step in sends:
+
+        @pl.when(direct(step))
+        def _():
+            make(step).wait_send()
+
+    for side, delta in enumerate(SIDES):
+
+        @pl.when(has((delta, 0)) & paired)
+        def _():
+            for kind in range(2):
+                via_copy(kind, side).wait_send()
 
 
 def rest(
@@ -505,7 +632,7 @@
         return -(-count // SUB) * SUB
 
     edge, corner = whole(3 * rows * HORIZON), whole(3 * HORIZON * HORIZON)
-    edge_vol, corner_vol = whole(rows * WIDE), whole(WIDE * WIDE)
+    edge_vol, corner_vol = whole(rows * WIDE), whole(HORIZON * WIDE)
 
     def scratch(*shape):
         return pltpu.VMEM(shape + (depth,), jnp.float32)
@@ -536,14 +663,19 @@
             pltpu.VMEM((rows, cols), jnp.int32),
             scratch(2, edge_vol),
             scratch(4, corner_vol),
+            scratch(4, corner_vol),
             scratch(2, edge),
             scratch(4, corner),
             scratch(2, edge_vol),
             scratch(4, corner_vol),
+            scratch(4, corner_vol),
             scratch(2, 3, HORIZON, cols),
             scratch(2, edge),
             scratch(4, corner),
-            pltpu.SemaphoreType.DMA((4, len(STEPS))),
+            scratch(2, edge_vol),
+            scratch(2, edge),
+            pltpu.SemaphoreType.DMA((6, len(STEPS))),
+            pltpu.SemaphoreType.DMA((4, 2)),
             pltpu.SemaphoreType.DMA((4,)),
         ],
         compiler_params=pltpu.CompilerParams(

time: 32.1 us -> 30.4 us (0.947)
  Pallas kernels: 30.9 us -> 29.2 us
    pallas_call x1, Pallas kernels: 17.6 us -> 15.9 us  [shards(): pl.pallas_call(kernel, out_shape=(held(wide_rows, wide_cols), held(6, nea...]
where the time goes in v3:
time: 30.4 us; the launch traced here: 29.8 us
  Pallas kernels  29.2 us (96%)
  between operations  0.64 us (2%)
    pallas_call x1, Pallas kernels, shards(): pl.pallas_call(kernel, out_shape=(held(wide_rows, wide_cols), held(6, nea...  15.9 us
    pallas_call x1, Pallas kernels, shards(): pl.pallas_call(rest, out_shape=(result, result), in_specs=[vmem] * 4, out...  13.3 us

profile of v3, /device:TPU:27, one launch (start us, length us, event | category | flops | bytes accessed | tf_op | source)
XLA Modules:
  0.0 29.8 jit_solution(3574790109151626051)
XLA Ops:
  0.6 15.9 %gather.1 = (f32[20,48,128]{2,1,0:T(8,128)S(1)}, f32[6,14,48,128]{3,2,1,0:T(8,128)S(1)}, f32[6,6,8,48,128]{4,3,2,1,0:T(8,128)S(1)}, f32[3,7,2,32,128]{4,3,2,1,0:T(8,128)S(1)}) custom-call(f32[3,8,32,128]{3,2,1,0:T(8,128)} %disp_in.1, f32[8,32,128]{2,1,0:T(8,128)} %volume_in.1, s32[8,32]{1,0:T(8,128)} %material_in.1, s32[8,32]{1,0:T(8,128)} %layers_in.1), custom_call_target="tpu_custom_call" | custom-call | tf_op jit(solution)/shard_map/gather/pallas_call | solution.py:649
  16.5 13.3 %rest.1 = (f32[3,8,32,128]{3,2,1,0:T(8,128)}, f32[3,8,32,128]{3,2,1,0:T(8,128)}) custom-call(f32[20,48,128]{2,1,0:T(8,128)S(1)} %get-tuple-element.6.vol_ext, f32[6,14,48,128]{3,2,1,0:T(8,128)S(1)} %get-tuple-element.7.ext, f32[6,6,8,48,128]{4,3,2,1,0:T(8,128)S(1)} %get-tuple-element.8.mine, f32[3,7,2,32,128]{4,3,2,1,0:T(8,128)S(1)} %get-tuple-element.9.early), custom_call_target="tpu_custom_call" | custom-call | tf_op jit(solution)/shard_map/rest/pallas_call | solution.py:686

commit v4 on v3

--- a/solution.py
+++ b/solution.py
@@ -57,9 +57,44 @@
     return lax.rem(index + HORIZON, rows)
 
 
-def force_tile(vol_ext, ext, mine, sums, y, slot, tile):
+def known_bonds():
+    return [bond for bond in bond_list() if abs(bond[1]) < HORIZON]
+
+
+def bond_scale(kind):
+    square = sum(a * a for a in kind)
+    length = math.sqrt(square)
+    scale = 0.5 if sum(a > 0 for a in kind) == 1 else length / (2.0 * math.gcd(*kind))
+    return STIFF * influence(square) * scale, length
+
+
+def stretch_tile(vol_ext, ext, mine, known, y, slot, tile):
     start = pl.multiple_of(tile * SUB, SUB)
     row = y + HORIZON
+    own = {}
+    for index, bond in enumerate(known_bonds()):
+        ox, oy, oz = bond
+        at = pl.ds(start + (SUB + ox), SUB)
+        apart = []
+        for k in range(3):
+            if (k, oz) not in own:
+                if oz:
+                    own[k, oz] = mine[k, AWAY.index(oz), y, pl.ds(start + SUB, SUB), :]
+                else:
+                    own[k, oz] = ext[k, row, pl.ds(start + SUB, SUB), :]
+            apart.append(ext[k, row + oy, at, :] - own[k, oz])
+        squared = apart[0] * apart[0] + apart[1] * apart[1] + apart[2] * apart[2]
+        scale, length = bond_scale(tuple(sorted(map(abs, bond))))
+        pull = scale / length - scale * lax.rsqrt(squared)
+        pull = pull * vol_ext[row + HORIZON + oy, at, :]
+        for k in range(3):
+            known[slot, index, k] = pull * apart[k]
+
+
+def force_tile(vol_ext, ext, mine, sums, y, slot, tile, known=None, place=None):
+    start = pl.multiple_of(tile * SUB, SUB)
+    row = y + HORIZON
+    stored = known_bonds()
 
     def load(field, ox, oy):
         at = pl.ds(start + (SUB + ox), SUB)
@@ -83,22 +118,13 @@
                 sums[k] = term if sums[k] is None else sums[k] + term
 
         for kind, bonds in kinds.items():
-            square = sum(a * a for a in kind)
-            length = math.sqrt(square)
+            scale, length = bond_scale(kind)
             common = math.gcd(*kind)
             count = sum(a > 0 for a in kind)
-            scale = 0.5 if count == 1 else length / (2.0 * common)
-            scale = STIFF * influence(square) * scale
-            late = len(bonds) > 6
+            late = len(bonds) > 6 and known is None
             total = [None, None, None]
             for bond in bonds:
                 ox, oy, _ = bond
-                apart = [load(k, ox, oy) - own[k] for k in range(3)]
-                squared = apart[0] * apart[0] + apart[1] * apart[1] + apart[2] * apart[2]
-                if late:
-                    pull = 1.0 / length - lax.rsqrt(squared)
-                else:
-                    pull = scale / length - scale * lax.rsqrt(squared)
                 near = [k for k in range(3) if bond[k]]
                 pair = {k: own[3 + k] + load(3 + k, ox, oy) for k in near}
                 if count == 1:
@@ -123,6 +149,16 @@
                         if part[a] != 1:
                             second = second * float(part[a])
                         ratio = pair[a] * pair[b] * pair[odd] * lax.rsqrt(first + second)
+                if known is not None and bond in stored:
+                    index = stored.index(bond)
+                    add(summed, ratio, [known[place, index, k] for k in range(3)])
+                    continue
+                apart = [load(k, ox, oy) - own[k] for k in range(3)]
+                squared = apart[0] * apart[0] + apart[1] * apart[1] + apart[2] * apart[2]
+                if late:
+                    pull = 1.0 / length - lax.rsqrt(squared)
+                else:
+                    pull = scale / length - scale * lax.rsqrt(squared)
                 factor = (ratio * pull) * load(6, ox, oy)
                 add(total if late else summed, factor, apart)
             if late:
@@ -132,7 +168,7 @@
 
 
 def kernel(
-    disp_in, volume_in, material_in, layers_in, vol_ext, ext, mine, sums,
+    disp_in, volume_in, material_in, layers_in, vol_ext, ext, mine, sums, known,
     disp, volume, material, layers,
     send_xv, send_cn, send_cf, send_x, send_c, got_xv, got_cn, got_cf, got_y, got_x, got_c,
     via_xv, via_x, sems, via_sems, load_sems,
@@ -536,19 +572,29 @@
     early = rows - 2 * HORIZON
     inner = own_tiles - 2
 
-    def tile_step(i, carry):
-        @pl.when(i == early * inner)
-        def _():
-            edges()
-
-        later = i - early * inner
-        slot = jnp.where(later < 0, lax.div(i, inner), lax.div(later, 2))
-        tile = jnp.where(later < 0, lax.rem(i, inner) + 1, lax.rem(later, 2) * (own_tiles - 1))
-        force_tile(vol_ext, ext, mine, sums, middle_row(rows, slot), slot, tile)
+    def stretch_step(i, carry):
+        y = lax.div(i, inner) + (HORIZON - 1)
+        stretch_tile(vol_ext, ext, mine, known, y, i, lax.rem(i, inner) + 1)
         return carry
 
+    def middle_step(i, carry):
+        slot = lax.div(i, inner)
+        tile = lax.rem(i, inner) + 1
+        y = slot + HORIZON
+        force_tile(vol_ext, ext, mine, sums, y, slot, tile, known, i + inner)
+        return carry
+
+    def edge_step(i, carry):
+        slot = lax.div(i, 2)
+        tile = lax.rem(i, 2) * (own_tiles - 1)
+        force_tile(vol_ext, ext, mine, sums, slot + HORIZON, slot, tile)
+        return carry
+
+    lax.fori_loop(0, (early + 2) * inner, stretch_step, 0)
     middle()
-    lax.fori_loop(0, early * own_tiles, tile_step, 0)
+    lax.fori_loop(0, early * inner, middle_step, 0)
+    edges()
+    lax.fori_loop(0, early * 2, edge_step, 0)
     for step in (*CORNERS, *along_y):
         arrived(far_copy, step)
     fill_corners(got_cf, far_row, far_halo)
@@ -574,7 +620,7 @@
 
 
 def rest(
-    vol_ext, ext, mine, early, fac_out, force_out, sums, force, out_sems, fac_sem
+    vol_ext, ext, mine, early, known, fac_out, force_out, sums, force, out_sems, fac_sem
 ):
     rows, cols = force.shape[1], force.shape[2]
     lane = lax.broadcasted_iota(jnp.int32, (SUB, LANES), 1)
@@ -582,7 +628,9 @@
     fac_copy = pltpu.make_async_copy(own, fac_out, fac_sem)
     fac_copy.start()
     done = early.shape[2]
-    half = sums.shape[2]
+    count = sums.shape[2]
+    half = count // 2
+    each = (count * (cols // SUB) - 2 * (cols // SUB - 2)) // 2
 
     def out_copy(y):
         return pltpu.make_async_copy(force.at[:, y], force_out.at[:, y], out_sems.at[y])
@@ -598,24 +646,37 @@
                 force[k, y, at : at + SUB, :] = jnp.where(alive, total, 0.0)
         out_copy(y).start()
 
-    def group(first, carry):
-        def row(slot, inner):
-            y = middle_row(rows, first * half + slot + done)
-
-            def one(tile, last):
-                force_tile(vol_ext, ext, mine, sums, y, slot, tile)
-                return last
-
-            return lax.fori_loop(0, cols // SUB, one, inner)
-
-        lax.fori_loop(0, half, row, 0)
+    tiles = cols // SUB
+    inner = tiles - 2
+
+    def middle_step(i, carry):
+        end = lax.div(i, inner)
+        tile = lax.rem(i, inner)
+        y = jnp.where(end == 0, HORIZON + done, HORIZON - 1)
+        place = jnp.where(end == 0, (done + 1) * inner, 0) + tile
+        force_tile(vol_ext, ext, mine, sums, y, end * (count - 1), tile + 1, known, place)
+        return carry
+
+    def group(part, carry):
+        def step(j, last):
+            i = part * each + j
+            between = lax.rem(i + (tiles - 2), tiles)
+            end = (i < 2) | (i >= 2 * each - 2)
+            slot = lax.div(i + (tiles - 2), tiles)
+            tile = jnp.where(end, lax.rem(i, 2) * (tiles - 1), between)
+            force_tile(vol_ext, ext, mine, sums, middle_row(rows, slot + done), slot, tile)
+            return last
+
+        lax.fori_loop(0, each, step, carry)
         for slot in range(half):
-            finish(sums, slot, middle_row(rows, first * half + slot + done))
+            at = part * half + slot
+            finish(sums, at, middle_row(rows, at + done))
         return carry
 
     for slot in range(done):
         finish(early, slot, (slot + HORIZON) % rows)
-    lax.fori_loop(0, (rows - done) // half, group, 0)
+    lax.fori_loop(0, 2 * inner, middle_step, 0)
+    lax.fori_loop(0, 2, group, 0)
     fac_copy.wait()
     for y in range(rows):
         out_copy(y).wait()
@@ -653,9 +714,10 @@
             held(6, near_rows, wide_cols),
             held(6, len(AWAY), rows, wide_cols),
             held(3, frames, early, cols),
+            held((early + 2) * (cols // SUB - 2), len(known_bonds()), 3, SUB),
         ),
         in_specs=[hbm] * 4,
-        out_specs=(vmem,) * 4,
+        out_specs=(vmem,) * 5,
         scratch_shapes=[
             scratch(3, rows, cols),
             scratch(rows, cols),
@@ -686,10 +748,10 @@
     return pl.pallas_call(
         rest,
         out_shape=(result, result),
-        in_specs=[vmem] * 4,
+        in_specs=[vmem] * 5,
         out_specs=(hbm, hbm),
         scratch_shapes=[
-            scratch(3, frames, HORIZON, cols),
+            scratch(3, frames, rows - early, cols),
             scratch(3, rows, cols),
             pltpu.SemaphoreType.DMA((rows,)),
             pltpu.SemaphoreType.DMA,

time: 30.4 us -> 28.9 us (0.951)
  the two profiles are of different devices: /device:TPU:27 before, /device:TPU:58 now
where the time goes in v4:
time: 28.9 us; the launch traced here: 28.7 us
  Pallas kernels  28.1 us (97%)
  between operations  0.64 us (2%)
    pallas_call x1, Pallas kernels, shards(): pl.pallas_call(kernel, out_shape=(held(wide_rows, wide_cols), held(6, nea...  15.4 us
    pallas_call x1, Pallas kernels, shards(): pl.pallas_call(rest, out_shape=(result, result), in_specs=[vmem] * 5, out...  12.7 us

profile of v4, /device:TPU:58, one launch (start us, length us, event | category | flops | bytes accessed | tf_op | source)
XLA Modules:
  0.0 28.7 jit_solution(14885819206137756913)
XLA Ops:
  0.6 15.4 %gather.1 = (f32[20,48,128]{2,1,0:T(8,128)S(1)}, f32[6,14,48,128]{3,2,1,0:T(8,128)S(1)}, f32[6,6,8,48,128]{4,3,2,1,0:T(8,128)S(1)}, f32[3,7,2,32,128]{4,3,2,1,0:T(8,128)S(1)}, f32[8,120,3,8,128]{4,3,2,1,0:T(8,128)S(1)}) custom-call(f32[3,8,32,128]{3,2,1,0:T(8,128)} %disp_in.1, f32[8,32,128]{2,1,0:T(8,128)} %volume_in.1, s32[8,32]{1,0:T(8,128)} %material_in.1, ...), custom_call_target="tpu_custom_call" | custom-call | tf_op jit(solution)/shard_map/gather/pallas_call | solution.py:710
  16.1 12.7 %rest.1 = (f32[3,8,32,128]{3,2,1,0:T(8,128)}, f32[3,8,32,128]{3,2,1,0:T(8,128)}) custom-call(f32[20,48,128]{2,1,0:T(8,128)S(1)} %get-tuple-element.7.vol_ext, f32[6,14,48,128]{3,2,1,0:T(8,128)S(1)} %get-tuple-element.8.ext, f32[6,6,8,48,128]{4,3,2,1,0:T(8,128)S(1)} %get-tuple-element.9.mine, f32[3,7,2,32,128]{4,3,2,1,0:T(8,128)S(1)} %get-tuple-element.10.early, ...), custom_call_target="tpu_custom_call" | custom-call | tf_op jit(solution)/shard_map/rest/pallas_call | solution.py:748

commit v5 on v4

--- a/solution.py
+++ b/solution.py
@@ -11,7 +11,7 @@
 STIFF = 5.0
 WIDE = 2 * HORIZON
 LANES = 128
-VMEM_LIMIT = 24 * 2**20
+VMEM_LIMIT = 16 * 2**20
 SUB = 8
 MESH = pl.DeviceIdType.MESH
 SIDES = (-1, 1)
@@ -57,8 +57,14 @@
     return lax.rem(index + HORIZON, rows)
 
 
-def known_bonds():
-    return [bond for bond in bond_list() if abs(bond[1]) < HORIZON]
+def within(rows, side=0):
+    return [bond for bond in bond_list() if abs(bond[1]) <= rows and side * bond[0] <= 0]
+
+
+MIDDLE = within(HORIZON - 1)
+LEFT = within(HORIZON - 1, -1)
+RIGHT = within(HORIZON - 1, 1)
+BESIDE = within(HORIZON - 2)
 
 
 def bond_scale(kind):
@@ -68,11 +74,11 @@
     return STIFF * influence(square) * scale, length
 
 
-def stretch_tile(vol_ext, ext, mine, known, y, slot, tile):
+def stretch_tile(vol_ext, ext, mine, known, bonds, y, slot, tile):
     start = pl.multiple_of(tile * SUB, SUB)
     row = y + HORIZON
     own = {}
-    for index, bond in enumerate(known_bonds()):
+    for index, bond in enumerate(bonds):
         ox, oy, oz = bond
         at = pl.ds(start + (SUB + ox), SUB)
         apart = []
@@ -91,10 +97,9 @@
             known[slot, index, k] = pull * apart[k]
 
 
-def force_tile(vol_ext, ext, mine, sums, y, slot, tile, known=None, place=None):
+def force_tile(vol_ext, ext, mine, sums, y, slot, tile, known=None, stored=(), place=None):
     start = pl.multiple_of(tile * SUB, SUB)
     row = y + HORIZON
-    stored = known_bonds()
 
     def load(field, ox, oy):
         at = pl.ds(start + (SUB + ox), SUB)
@@ -121,7 +126,8 @@
             scale, length = bond_scale(kind)
             common = math.gcd(*kind)
             count = sum(a > 0 for a in kind)
-            late = len(bonds) > 6 and known is None
+            fresh = [bond for bond in bonds if bond not in stored]
+            late = len(fresh) > 6
             total = [None, None, None]
             for bond in bonds:
                 ox, oy, _ = bond
@@ -149,7 +155,7 @@
                         if part[a] != 1:
                             second = second * float(part[a])
                         ratio = pair[a] * pair[b] * pair[odd] * lax.rsqrt(first + second)
-                if known is not None and bond in stored:
+                if bond in stored:
                     index = stored.index(bond)
                     add(summed, ratio, [known[place, index, k] for k in range(3)])
                     continue
@@ -167,9 +173,22 @@
             sums[k, oz + HORIZON, slot, pl.ds(start, SUB), :] = summed[k]
 
 
+def finish_row(vol_ext, parts, slot, y, force, at_row):
+    lane = lax.broadcasted_iota(jnp.int32, (SUB, LANES), 1)
+    for at in range(0, force.shape[2], SUB):
+        alive = vol_ext[y + WIDE, SUB + at : 2 * SUB + at, :] > 0
+        for k in range(3):
+            total = parts[k, HORIZON, slot, at : at + SUB, :]
+            for oz in AWAY:
+                part = moved(parts[k, oz + HORIZON, slot, at : at + SUB, :], oz)
+                total = total + jnp.where(inside(lane, oz), part, 0.0)
+            force[k, at_row, at : at + SUB, :] = jnp.where(alive, total, 0.0)
+
+
 def kernel(
-    disp_in, volume_in, material_in, layers_in, vol_ext, ext, mine, sums, known,
-    disp, volume, material, layers,
+    disp_in, volume_in, material_in, layers_in, vol_ext, ext, mine, first_force,
+    known, known_left, known_right, known_beside,
+    sums, disp, volume, material, layers,
     send_xv, send_cn, send_cf, send_x, send_c, got_xv, got_cn, got_cf, got_y, got_x, got_c,
     via_xv, via_x, sems, via_sems, load_sems,
 ):
@@ -329,6 +348,18 @@
         return carry
 
     lax.fori_loop(0, rows, own_row, 0)
+
+    own_tiles = cols // SUB
+    early = rows - 2 * HORIZON
+    inner = own_tiles - 2
+
+    def stretch_ends(i, carry):
+        y = i + (HORIZON - 1)
+        stretch_tile(vol_ext, ext, mine, known_left, LEFT, y, i, 0)
+        stretch_tile(vol_ext, ext, mine, known_right, RIGHT, y, i, own_tiles - 1)
+        return carry
+
+    lax.fori_loop(0, early + 2, stretch_ends, 0)
 
     peers = sum(direct(step).astype(jnp.int32) for step in STEPS)
     pl.semaphore_wait(barrier, peers)
@@ -508,8 +539,6 @@
         lax.fori_loop(0, rows // 4, factor_rows(HORIZON, 1, 4, 4, near), 0)
         lax.fori_loop(0, rows // 4, factor_moved(own), 0)
 
-    own_tiles = cols // SUB
-
     def middle():
         for step in along_y:
             arrived(vol_copy, step)
@@ -569,36 +598,44 @@
 
         lax.fori_loop(0, HORIZON, halo_row, 0)
 
-    early = rows - 2 * HORIZON
-    inner = own_tiles - 2
-
-    def stretch_step(i, carry):
+    def stretch_middle(i, carry):
         y = lax.div(i, inner) + (HORIZON - 1)
-        stretch_tile(vol_ext, ext, mine, known, y, i, lax.rem(i, inner) + 1)
+        stretch_tile(vol_ext, ext, mine, known, MIDDLE, y, i, lax.rem(i, inner) + 1)
+        return carry
+
+    def stretch_beside(i, carry):
+        y = (HORIZON - 2) + lax.div(i, inner) * (early + 3)
+        stretch_tile(vol_ext, ext, mine, known_beside, BESIDE, y, i, lax.rem(i, inner) + 1)
         return carry
 
     def middle_step(i, carry):
         slot = lax.div(i, inner)
         tile = lax.rem(i, inner) + 1
         y = slot + HORIZON
-        force_tile(vol_ext, ext, mine, sums, y, slot, tile, known, i + inner)
+        force_tile(vol_ext, ext, mine, sums, y, slot, tile, known, MIDDLE, i + inner)
         return carry
 
-    def edge_step(i, carry):
-        slot = lax.div(i, 2)
-        tile = lax.rem(i, 2) * (own_tiles - 1)
-        force_tile(vol_ext, ext, mine, sums, slot + HORIZON, slot, tile)
-        return carry
-
-    lax.fori_loop(0, (early + 2) * inner, stretch_step, 0)
+    def end_step(tile, terms, stored):
+        def body(slot, carry):
+            y = slot + HORIZON
+            force_tile(vol_ext, ext, mine, sums, y, slot, tile, terms, stored, slot + 1)
+            return carry
+
+        return body
+
+    lax.fori_loop(0, (early + 2) * inner, stretch_middle, 0)
+    lax.fori_loop(0, 2 * inner, stretch_beside, 0)
     middle()
     lax.fori_loop(0, early * inner, middle_step, 0)
     edges()
-    lax.fori_loop(0, early * 2, edge_step, 0)
+    lax.fori_loop(0, early, end_step(0, known_left, LEFT), 0)
+    lax.fori_loop(0, early, end_step(own_tiles - 1, known_right, RIGHT), 0)
     for step in (*CORNERS, *along_y):
         arrived(far_copy, step)
     fill_corners(got_cf, far_row, far_halo)
     lax.fori_loop(0, HORIZON, factor_rows(0, rows + HORIZON, 1, 2, range(near_tiles)), 0)
+    for slot in range(early):
+        finish_row(vol_ext, sums, slot, slot + HORIZON, first_force, slot)
     for step in (*CORNERS, *along_y):
         arrived(disp_copy, step)
     handed(1)
@@ -620,41 +657,55 @@
 
 
 def rest(
-    vol_ext, ext, mine, early, known, fac_out, force_out, sums, force, out_sems, fac_sem
+    vol_ext, ext, mine, first_force, known, known_left, known_right, known_beside,
+    fac_out, force_out, sums, force, out_sems, fac_sem,
 ):
     rows, cols = force.shape[1], force.shape[2]
-    lane = lax.broadcasted_iota(jnp.int32, (SUB, LANES), 1)
     own = ext.at[3:6, HORIZON : HORIZON + rows, SUB : SUB + cols]
-    fac_copy = pltpu.make_async_copy(own, fac_out, fac_sem)
-    fac_copy.start()
-    done = early.shape[2]
+    done = first_force.shape[1]
+    starts = [
+        pltpu.make_async_copy(own, fac_out, fac_sem.at[0]),
+        pltpu.make_async_copy(
+            first_force, force_out.at[:, HORIZON : HORIZON + done], fac_sem.at[1]
+        ),
+    ]
+    for copy in starts:
+        copy.start()
     count = sums.shape[2]
     half = count // 2
-    each = (count * (cols // SUB) - 2 * (cols // SUB - 2)) // 2
+    tiles = cols // SUB
+    inner = tiles - 2
+    each = tiles + 2
 
     def out_copy(y):
         return pltpu.make_async_copy(force.at[:, y], force_out.at[:, y], out_sems.at[y])
-
-    def finish(parts, slot, y):
-        for at in range(0, cols, SUB):
-            alive = vol_ext[y + WIDE, SUB + at : 2 * SUB + at, :] > 0
-            for k in range(3):
-                total = parts[k, HORIZON, slot, at : at + SUB, :]
-                for oz in AWAY:
-                    part = moved(parts[k, oz + HORIZON, slot, at : at + SUB, :], oz)
-                    total = total + jnp.where(inside(lane, oz), part, 0.0)
-                force[k, y, at : at + SUB, :] = jnp.where(alive, total, 0.0)
-        out_copy(y).start()
-
-    tiles = cols // SUB
-    inner = tiles - 2
 
     def middle_step(i, carry):
         end = lax.div(i, inner)
         tile = lax.rem(i, inner)
         y = jnp.where(end == 0, HORIZON + done, HORIZON - 1)
         place = jnp.where(end == 0, (done + 1) * inner, 0) + tile
-        force_tile(vol_ext, ext, mine, sums, y, end * (count - 1), tile + 1, known, place)
+        slot = end * (count - 1)
+        force_tile(vol_ext, ext, mine, sums, y, slot, tile + 1, known, MIDDLE, place)
+        return carry
+
+    def end_step(tile, terms, stored):
+        def body(end, carry):
+            y = jnp.where(end == 0, HORIZON + done, HORIZON - 1)
+            place = jnp.where(end == 0, done + 1, 0)
+            slot = end * (count - 1)
+            force_tile(vol_ext, ext, mine, sums, y, slot, tile, terms, stored, place)
+            return carry
+
+        return body
+
+    def beside_step(i, carry):
+        end = lax.div(i, inner)
+        tile = lax.rem(i, inner)
+        y = jnp.where(end == 0, HORIZON + done + 1, HORIZON - 2)
+        place = jnp.where(end == 0, inner, 0) + tile
+        slot = jnp.where(end == 0, 1, count - 2)
+        force_tile(vol_ext, ext, mine, sums, y, slot, tile + 1, known_beside, BESIDE, place)
         return carry
 
     def group(part, carry):
@@ -662,24 +713,28 @@
             i = part * each + j
             between = lax.rem(i + (tiles - 2), tiles)
             end = (i < 2) | (i >= 2 * each - 2)
-            slot = lax.div(i + (tiles - 2), tiles)
+            slot = lax.div(i + (tiles - 2), tiles) + 1
             tile = jnp.where(end, lax.rem(i, 2) * (tiles - 1), between)
             force_tile(vol_ext, ext, mine, sums, middle_row(rows, slot + done), slot, tile)
             return last
 
         lax.fori_loop(0, each, step, carry)
-        for slot in range(half):
-            at = part * half + slot
-            finish(sums, at, middle_row(rows, at + done))
+        for index in range(half):
+            slot = part * half + index
+            y = middle_row(rows, slot + done)
+            finish_row(vol_ext, sums, slot, y, force, y)
+            out_copy(y).start()
         return carry
 
-    for slot in range(done):
-        finish(early, slot, (slot + HORIZON) % rows)
     lax.fori_loop(0, 2 * inner, middle_step, 0)
+    lax.fori_loop(0, 2, end_step(0, known_left, LEFT), 0)
+    lax.fori_loop(0, 2, end_step(tiles - 1, known_right, RIGHT), 0)
+    lax.fori_loop(0, 2 * inner, beside_step, 0)
     lax.fori_loop(0, 2, group, 0)
-    fac_copy.wait()
-    for y in range(rows):
-        out_copy(y).wait()
+    for copy in starts:
+        copy.wait()
+    for index in range(count):
+        out_copy((index + done + HORIZON) % rows).wait()
 
 
 def shards(displacement, volume, material, layers):
@@ -713,12 +768,16 @@
             held(wide_rows, wide_cols),
             held(6, near_rows, wide_cols),
             held(6, len(AWAY), rows, wide_cols),
-            held(3, frames, early, cols),
-            held((early + 2) * (cols // SUB - 2), len(known_bonds()), 3, SUB),
+            held(3, early, cols),
+            held((early + 2) * (cols // SUB - 2), len(MIDDLE), 3, SUB),
+            held(early + 2, len(LEFT), 3, SUB),
+            held(early + 2, len(RIGHT), 3, SUB),
+            held(2 * (cols // SUB - 2), len(BESIDE), 3, SUB),
         ),
         in_specs=[hbm] * 4,
-        out_specs=(vmem,) * 5,
+        out_specs=(vmem,) * 8,
         scratch_shapes=[
+            scratch(3, frames, early, cols),
             scratch(3, rows, cols),
             scratch(rows, cols),
             pltpu.VMEM((rows, cols), jnp.int32),
@@ -748,13 +807,13 @@
     return pl.pallas_call(
         rest,
         out_shape=(result, result),
-        in_specs=[vmem] * 5,
+        in_specs=[vmem] * 8,
         out_specs=(hbm, hbm),
         scratch_shapes=[
             scratch(3, frames, rows - early, cols),
             scratch(3, rows, cols),
             pltpu.SemaphoreType.DMA((rows,)),
-            pltpu.SemaphoreType.DMA,
+            pltpu.SemaphoreType.DMA((2,)),
         ],
         compiler_params=pltpu.CompilerParams(vmem_limit_bytes=VMEM_LIMIT),
         name="rest",

time: 28.9 us -> 28.5 us (0.986)
  the two profiles are of different devices: /device:TPU:58 before, /device:TPU:121 now
where the time goes in v5:
time: 28.5 us; the launch traced here: 28.4 us
  Pallas kernels  27.8 us (98%)
  between operations  0.64 us (2%)
    pallas_call x1, Pallas kernels, shards(): pl.pallas_call(kernel, out_shape=(held(wide_rows, wide_cols), held(6, nea...  16.3 us
    pallas_call x1, Pallas kernels, shards(): pl.pallas_call(rest, out_shape=(result, result), in_specs=[vmem] * 8, out...  11.4 us

profile of v5, /device:TPU:121, one launch (start us, length us, event | category | flops | bytes accessed | tf_op | source)
XLA Modules:
  0.0 28.4 jit_solution(16505559479307327287)
XLA Ops:
  0.6 16.3 %gather.1 = (f32[20,48,128]{2,1,0:T(8,128)S(1)}, f32[6,14,48,128]{3,2,1,0:T(8,128)S(1)}, f32[6,6,8,48,128]{4,3,2,1,0:T(8,128)S(1)}, f32[3,2,32,128]{3,2,1,0:T(8,...) custom-call(f32[3,8,32,128]{3,2,1,0:T(8,128)} %disp_in.1, ...), custom_call_target="tpu_custom_call" | custom-call | tf_op jit(solution)/shard_map/gather/pallas_call | solution.py:765
  17.0 11.4 %rest.1 = (f32[3,8,32,128]{3,2,1,0:T(8,128)}, f32[3,8,32,128]{3,2,1,0:T(8,128)}) custom-call(f32[20,48,128]{2,1,0:T(8,128)S(1)} %get-tuple-element.10.vol_ext, f32[6,14,48,128]{3,2,1,0:T(8,128)S(1)} %get-tuple-element.11.ext, f32[6,6,8,48,128]{4,3,2,1,0:T(8,128)S(1)} %get-tuple-element.12.mine, f32[3,2,32,128]{3,2,1,0:T(8,128)S(1)} %get-tuple-element.13.first_force, ...), custom_call_target="tpu_custom_call" | custom-call | tf_op jit(solution)/shard_map/rest/pallas_call | solution.py:807

commit v6 on v5

--- a/solution.py
+++ b/solution.py
@@ -359,7 +359,6 @@
         stretch_tile(vol_ext, ext, mine, known_right, RIGHT, y, i, own_tiles - 1)
         return carry
 
-    lax.fori_loop(0, early + 2, stretch_ends, 0)
 
     peers = sum(direct(step).astype(jnp.int32) for step in STEPS)
     pl.semaphore_wait(barrier, peers)
@@ -623,6 +622,7 @@
 
         return body
 
+    lax.fori_loop(0, early + 2, stretch_ends, 0)
     lax.fori_loop(0, (early + 2) * inner, stretch_middle, 0)
     lax.fori_loop(0, 2 * inner, stretch_beside, 0)
     middle()

time: 28.5 us -> 28 us (0.982)
  the two profiles are of different devices: /device:TPU:121 before, /device:TPU:1 now
where the time goes in v6:
time: 28 us; the launch traced here: 27.9 us
  Pallas kernels  27.2 us (97%)
  between operations  0.64 us (2%)
    pallas_call x1, Pallas kernels, shards(): pl.pallas_call(kernel, out_shape=(held(wide_rows, wide_cols), held(6, nea...  15.8 us
    pallas_call x1, Pallas kernels, shards(): pl.pallas_call(rest, out_shape=(result, result), in_specs=[vmem] * 8, out...  11.4 us

profile of v6, /device:TPU:1, one launch (start us, length us, event | category | flops | bytes accessed | tf_op | source)
XLA Modules:
  0.0 27.9 jit_solution(12442371157131301304)
XLA Ops:
  0.6 15.8 %gather.1 = (f32[20,48,128]{2,1,0:T(8,128)S(1)}, f32[6,14,48,128]{3,2,1,0:T(8,128)S(1)}, f32[6,6,8,48,128]{4,3,2,1,0:T(8,128)S(1)}, f32[3,2,32,128]{3,2,1,0:T(8,...) custom-call(f32[3,8,32,128]{3,2,1,0:T(8,128)} %disp_in.1, ...), custom_call_target="tpu_custom_call" | custom-call | tf_op jit(solution)/shard_map/gather/pallas_call | solution.py:765
  16.5 11.4 %rest.1 = (f32[3,8,32,128]{3,2,1,0:T(8,128)}, f32[3,8,32,128]{3,2,1,0:T(8,128)}) custom-call(f32[20,48,128]{2,1,0:T(8,128)S(1)} %get-tuple-element.10.vol_ext, f32[6,14,48,128]{3,2,1,0:T(8,128)S(1)} %get-tuple-element.11.ext, f32[6,6,8,48,128]{4,3,2,1,0:T(8,128)S(1)} %get-tuple-element.12.mine, f32[3,2,32,128]{3,2,1,0:T(8,128)S(1)} %get-tuple-element.13.first_force, ...), custom_call_target="tpu_custom_call" | custom-call | tf_op jit(solution)/shard_map/rest/pallas_call | solution.py:807
